TPU v7x, 128 devices: a whole 4x4x4 slice. The times are simulated.
128 devices in a mesh: req: 32 (over y, x, core), head: 4 (over z).
Axes of the slice: x: 4, y: 4, z: 4, core: 2. Of those that a mesh axis runs over, the one named last changes fastest.
Arguments:
- hidden_in: bfloat16 [1024, 5120], P('req'), may hold values from -60 to 60
- query: bfloat16 [1024, 4096], P('req', 'head'), may hold values from -12 to 12
- incoming_key: bfloat16 [1024, 1024], P('req', 'head'), may hold values from -6 to 6
- incoming_value: bfloat16 [1024, 1024], P('req', 'head'), may hold values from -6 to 6
- private_tail_keys: bfloat16 [1024, 160, 1024], P('req', None, 'head'), may hold values from -6 to 6
- private_tail_values: bfloat16 [1024, 160, 1024], P('req', None, 'head'), may hold values from -6 to 6
- group_prompt_keys: bfloat16 [96, 512, 1024], P('req', None, 'head'), may hold values from -6 to 6
- group_prompt_values: bfloat16 [96, 512, 1024], P('req', None, 'head'), may hold values from -6 to 6
- group_id: int32 [1024], P('req'), may hold values from 0 to 95, as said below
- prompt_len: int32 [96], P('req'), may hold values from 128 to 512, as said below
- tail_len: int32 [1024], P('req'), may hold values from 0 to 159, as said below
- out_proj: bfloat16 [4096, 5120], P('head'), may hold values from -0.5 to 0.5
- norm_gain: float32 [5120], replicated, may hold values from 0.1 to 1.9
- gate_proj: bfloat16 [5120, 32768], P(None, ('req', 'head')), may hold values from -0.078125 to 0.078125
- up_proj: bfloat16 [5120, 32768], P(None, ('req', 'head')), may hold values from -0.078125 to 0.078125
- down_proj: bfloat16 [32768, 5120], P('req', 'head'), may hold values from -0.03125 to 0.03125
Outputs:
- layer_out: bfloat16 [1024, 5120], P(('req', 'head'))
Inputs may be any that keep to these rules, and one draw needn't show every extreme that they name: `group_id`: the prompt cache of group g is held by index g // 3 of req. Among the 32 requests of one index of req, at most 2 belong to groups held by any one index of req; in every draw one index of req holds the groups of exactly 2 requests of every index of req. `prompt_len`: some group's prompt fills all 512 positions. Request r's earlier private tokens are in slots 0 to tail_len[r] - 1; some request has 159 of them.
All inputs are finite; a program needn't handle non-finite values.
Results may differ from a plain program's by a relative error of at most 0.007.
Values may be sent and summed in bfloat16 or wider, within the bound.
No kernel may reach another device: no remote copies, remote signals or barrier semaphores. Data moves between devices by JAX's collectives and lax.ppermute only.
A program may use at most 128 MiB of HBM per device.

v0:
```python
import jax
import jax.numpy as jnp
from jax import lax
from jax.sharding import PartitionSpec as P

QUERY_HEADS = 32
KEY_VALUE_HEADS = 8
HEAD_WIDTH = 128


MASKED_SCORE = -1e30


def shards(
    hidden_in,
    query,
    incoming_key,
    incoming_value,
    private_tail_keys,
    private_tail_values,
    group_prompt_keys,
    group_prompt_values,
    group_id,
    prompt_len,
    tail_len,
    out_proj,
    norm_gain,
    gate_proj,
    up_proj,
    down_proj,
):
    n_req = lax.axis_size("req")
    n_head = lax.axis_size("head")
    row_count = query.shape[0]
    kv_local = incoming_key.shape[1] // HEAD_WIDTH
    each_key_value = QUERY_HEADS // KEY_VALUE_HEADS
    group_count = prompt_len.shape[0]
    prompt_size = group_prompt_keys.shape[1]
    tail_size = private_tail_keys.shape[1]
    slot_cap = 2 * row_count // n_req
    slot_total = n_req * slot_cap
    scale_of_scores = HEAD_WIDTH ** (-0.5)
    col_width = query.shape[1]
    head_local = kv_local * each_key_value
    holder = group_id // group_count
    local_group = group_id - holder * group_count
    holder_hot = (holder[:, None] == jnp.arange(n_req)[None, :]).astype(jnp.int32)
    before = jnp.cumsum(holder_hot, axis=0) - holder_hot
    order_in = jnp.sum(before * holder_hot, axis=1)
    slot_of = holder * slot_cap + order_in
    placing = slot_of[:, None] == jnp.arange(slot_total)[None, :]
    send_query = (
        jnp.einsum(
            "rs,rc->sc", placing.astype(jnp.bfloat16), query, preferred_element_type=jnp.float32
        )
        .astype(jnp.bfloat16)
        .reshape(n_req, slot_cap, col_width)
    )
    send_group = (
        jnp.sum(placing.astype(jnp.int32) * (local_group[:, None] + 1), axis=0) - 1
    ).reshape(n_req, slot_cap)
    keys_all = group_prompt_keys.reshape(group_count * prompt_size, kv_local, HEAD_WIDTH)
    values_all = group_prompt_values.reshape(group_count * prompt_size, kv_local, HEAD_WIDTH)
    key_group = jnp.arange(group_count * prompt_size) // prompt_size
    key_live = jnp.arange(group_count * prompt_size) % prompt_size < jnp.repeat(
        prompt_len, prompt_size
    )
    recv_query = lax.all_to_all(send_query, "req", split_axis=0, concat_axis=0, tiled=True)
    recv_group = lax.all_to_all(send_group, "req", split_axis=0, concat_axis=0, tiled=True)
    sources, item_count = recv_group.shape
    flat_query = recv_query.reshape(sources * item_count, kv_local, each_key_value, HEAD_WIDTH)
    scores = (
        jnp.einsum("nkrd,pkd->nkrp", flat_query, keys_all, preferred_element_type=jnp.float32)
        * scale_of_scores
    )
    usable = (recv_group.reshape(sources * item_count)[:, None] == key_group[None, :]) & key_live[
        None, :
    ]
    masked = jnp.where(usable[:, None, None, :], scores, MASKED_SCORE)
    largest = jnp.max(masked, axis=-1)
    weights = jnp.exp(masked - largest[..., None])
    totals = jnp.sum(weights, axis=-1)
    mixture = jnp.einsum(
        "nkrp,pkd->nkrd",
        weights.astype(jnp.bfloat16),
        values_all,
        preferred_element_type=jnp.float32,
    )
    back_mix = lax.all_to_all(
        mixture.reshape(sources, item_count, col_width),
        "req",
        split_axis=0,
        concat_axis=0,
        tiled=True,
    )
    back_peak = lax.all_to_all(
        largest.reshape(sources, item_count, head_local),
        "req",
        split_axis=0,
        concat_axis=0,
        tiled=True,
    )
    back_total = lax.all_to_all(
        totals.reshape(sources, item_count, head_local),
        "req",
        split_axis=0,
        concat_axis=0,
        tiled=True,
    )
    shared_mix = jnp.take(back_mix.reshape(slot_total, col_width), slot_of, axis=0).reshape(
        row_count, kv_local, each_key_value, HEAD_WIDTH
    )
    shared_max = jnp.take(back_peak.reshape(slot_total, head_local), slot_of, axis=0).reshape(
        row_count, kv_local, each_key_value
    )
    shared_total = jnp.take(back_total.reshape(slot_total, head_local), slot_of, axis=0).reshape(
        row_count, kv_local, each_key_value
    )
    query_rows = query.reshape(row_count, kv_local, each_key_value, HEAD_WIDTH)
    request_keys = private_tail_keys.reshape(row_count, tail_size, kv_local, HEAD_WIDTH)
    request_values = private_tail_values.reshape(row_count, tail_size, kv_local, HEAD_WIDTH)
    tail_scores = (
        jnp.einsum("bkrd,btkd->bkrt", query_rows, request_keys, preferred_element_type=jnp.float32)
        * scale_of_scores
    )
    current_scores = (
        jnp.einsum(
            "ivxg,ivg->ivx",
            query_rows,
            incoming_key.reshape(row_count, kv_local, HEAD_WIDTH),
            preferred_element_type=jnp.float32,
        )
        * scale_of_scores
    )
    tail_live = (jnp.arange(tail_size)[None, :] < tail_len[:, None])[:, None, None, :]
    tail_masked = jnp.where(tail_live, tail_scores, MASKED_SCORE)
    local_max = jnp.maximum(jnp.max(tail_masked, axis=-1), current_scores)
    tail_exp = jnp.exp(tail_masked - local_max[..., None])
    fresh_exp = jnp.exp(current_scores - local_max)
    local_total = jnp.sum(tail_exp, axis=-1) + fresh_exp
    fresh_weights = lax.optimization_barrier(fresh_exp.astype(jnp.bfloat16)).astype(jnp.float32)
    fresh_vals = incoming_value.reshape(row_count, kv_local, HEAD_WIDTH).astype(jnp.float32)
    local_mix = (
        jnp.einsum(
            "bkrt,btkd->bkrd",
            tail_exp.astype(jnp.bfloat16),
            request_values,
            preferred_element_type=jnp.float32,
        )
        + fresh_weights[..., None] * fresh_vals[:, :, None, :]
    )
    highest = jnp.maximum(shared_max, local_max)
    shared_factor = jnp.exp(shared_max - highest)
    local_factor = jnp.exp(local_max - highest)
    numer = shared_mix * shared_factor[..., None] + local_mix * local_factor[..., None]
    denom = shared_total * shared_factor + local_total * local_factor
    attention = (numer / denom[..., None]).reshape(row_count, col_width).astype(jnp.bfloat16)
    projected = jnp.dot(attention, out_proj, preferred_element_type=jnp.float32)
    sub_rows = row_count // n_head
    head_index = lax.axis_index("head")
    summed = lax.psum(projected, "head")
    residual = (hidden_in.astype(jnp.float32) + summed).astype(jnp.bfloat16)
    resid_f = residual.astype(jnp.float32)
    segment = lax.all_gather(
        (
            resid_f
            * lax.rsqrt(jnp.mean(resid_f * resid_f, axis=-1, keepdims=True) + 1e-05)
            * norm_gain
        ).astype(jnp.bfloat16),
        "req",
        axis=0,
        tiled=True,
    )
    gate_vals = jnp.dot(segment, gate_proj, preferred_element_type=jnp.float32)
    up_vals = jnp.dot(segment, up_proj, preferred_element_type=jnp.float32)
    hidden = (jax.nn.silu(gate_vals) * up_vals).astype(jnp.bfloat16)
    own_rows = lax.dynamic_slice_in_dim(residual, head_index * sub_rows, sub_rows, 0)
    down_rows = lax.all_to_all(down_proj, "head", split_axis=0, concat_axis=1, tiled=True)
    lowered = lax.psum_scatter(
        jnp.dot(hidden, down_rows, preferred_element_type=jnp.float32),
        ("req", "head"),
        scatter_dimension=0,
        tiled=True,
    )
    return (own_rows.astype(jnp.float32) + lowered).astype(jnp.bfloat16)


def solution(mesh):
    return jax.shard_map(
        shards,
        mesh=mesh,
        in_specs=(
            P("req", None),
            P("req", "head"),
            P("req", "head"),
            P("req", "head"),
            P("req", None, "head"),
            P("req", None, "head"),
            P("req", None, "head"),
            P("req", None, "head"),
            P("req"),
            P("req"),
            P("req"),
            P("head", None),
            P(),
            P(None, ("req", "head")),
            P(None, ("req", "head")),
            P("req", "head"),
        ),
        out_specs=P(("req", "head"), None),
        check_vma=False,
    )
```

profile of v0, /device:TPU:0, one launch (start us, length us, event | category | flops | bytes accessed | tf_op | source)
XLA Modules:
  0.0 910.8 jit_solution(5117704881106043649)
XLA Ops:
  9.0 7.4 all-to-all-start
  17.0 1.1 convolution_convert_fusion
  18.1 0.9 reshape.209
  20.5 3.3 fusion.65
  24.9 0.9 fusion.43
  27.1 2.0 reshape.202
  29.2 7.5 all-to-all-start.1
  38.8 5.7 all-to-all-done.1
  44.5 1.6 reshape.201
  46.1 1.7 fusion.66
  47.9 1.6 copy-done.2
  51.0 3.9 all-to-all-start.4
  55.5 2.0 reshape.203
  59.8 2.5 all-to-all-done.4
  62.2 4.9 all-to-all-start.3
  67.2 2.6 fusion.20
  69.9 0.9 reshape.204
  71.5 3.0 all-to-all-done.3
  74.6 4.4 all-to-all-start.2
  82.0 5.8 all-to-all-done.2
  88.9 2.6 fusion.35
  91.6 6.8 fusion.68
  98.6 42.6 %all-reduce.2.cloned.1.call-done = f32[32,5120]{1,0:T(8,128)} async-done(((f32[32,5120]{1,0:T(8,128)}), f32[32,5120]{1,0:T(8,128)}) %all-reduce.2.cloned.1.call-update) | async-done | bytes 655376 | tf_op jit(solution)/shard_map/psum | solution.py:161
  141.2 1.3 fusion.40
  142.5 0.9 fusion.42
  143.4 35.0 %all_to_all.45 = bf16[4,256,1280]{2,1,0:T(8,128)(2,1)} all-to-all(bf16[4,256,1280]{2,1,0:T(8,128)(2,1)} %bitcast.79), channel_id=1, replica_groups=mesh['req'=32,'head'=4] {'head'}, dimensions={0} | all-to-all | bytes 5242880 | tf_op jit(solution)/shard_map/all_to_all | solution.py:178
  178.4 4.4 copy.99
  182.8 19.0 %all-gather.2.cloned.1.call-done = bf16[1024,5120]{1,0:T(8,128)(2,1)} async-done(((bf16[32,5120]{1,0:T(8,128)(2,1)}), bf16[1024,5120]{1,0:T(8,128)(2,1)}) %all-gather.2.cloned.1.call-update) | async-done | bytes 10485776 | tf_op jit(solution)/shard_map/all_gather | solution.py:164
  201.8 8.6 fusion.69
  210.4 18.4 %fusion.70 = f32[1024,5120]{1,0:T(8,128)} fusion(bf16[256,5120]{0,1:T(8,128)(2,1)} %bitcast.75, bf16[1024,5120]{1,0:T(8,128)(2,1)} %all-gather.2.cloned.1.call-done, bf16[5120,256]{1,0:T(8,128)(2,1)S(1)} %copy-done, f32[1024,256]{1,0:T(8,128)} %fusion.69), kind=kOutput, calls=%fused_computation.86 | convolution fusion | flops 5370281984 | bytes 37748736 | tf_op jit(solution)/shard_map/dot_general | solution.py:180
  228.8 673.9 %reduce-scatter.2.cloned.1.call-done = f32[8,5120]{1,0:T(8,128)} async-done(((f32[1024,5120]{1,0:T(8,128)}), f32[8,5120]{1,0:T(8,128)}) %reduce-scatter.2.cloned.1.call-update) | async-done | bytes 163856 | tf_op jit(solution)/shard_map/reduce_scatter | solution.py:179
  902.7 1.6 add_convert_fusion.1
  (79 shorter events, 18.7 us)
Async XLA Ops:
  6.5 203.8 %copy-start = (bf16[5120,256]{1,0:T(8,128)(2,1)S(1)}, bf16[5120,256]{1,0:T(8,128)(2,1)}, u32[]{:S(2)}) copy-start(bf16[5120,256]{1,0:T(8,128)(2,1)} %param.32) | copy-start | bytes 7864324
  6.5 17.4 %copy-start.8 = (bf16[32,256]{1,0:T(8,128)(2,1)S(1)}, bf16[32,256]{1,0:T(8,128)(2,1)}, u32[]{:S(2)}) copy-start(bf16[32,256]{1,0:T(8,128)(2,1)} %param.20) | copy-start | bytes 49156
  9.0 20.1 %all-to-all-start = ((s32[32,1,2]{2,1,0:T(1,128)}), s32[32,1,2]{2,1,0:T(1,128)S(1)}, u32[]{:S(2)}, u32[]{:S(2)}) async-start(s32[32,1,2]{2,1,0:T(1,128)} %bitcast), calls=%async_computation | async-start | bytes 32768 | tf_op jit(solution)/shard_map/all_to_all | solution.py:69
  23.8 2.6 copy-start.4
  29.2 15.3 %all-to-all-start.1 = ((bf16[32,2,1024]{2,1,0:T(2,128)(2,1)}), bf16[32,2,1024]{2,1,0:T(2,128)(2,1)}, u32[]{:S(2)}, u32[]{:S(2)}) async-start(bf16[32,2,1024]{2,1,0:T(2,128)(2,1)} %reshape.200), calls=%async_computation.1 | async-start | bytes 262144 | tf_op jit(solution)/shard_map/all_to_all | solution.py:68
  47.8 1.7 copy-start.2
  47.8 7.0 copy-start.11
  47.8 7.6 copy-start.6
  47.9 9.7 %copy-start.10 = (bf16[32,2,4]{0,2,1:T(4,128)(2,1)S(1)}, bf16[32,2,4]{0,2,1:T(4,128)(2,1)}, u32[]{:S(2)}) copy-start(bf16[32,2,4]{0,2,1:T(4,128)(2,1)} %get-tuple-element.8) | copy-start | bytes 1540
  47.9 10.4 %copy-start.9 = (bf16[32,256]{1,0:T(8,128)(2,1)S(1)}, bf16[32,256]{1,0:T(8,128)(2,1)}, u32[]{:S(2)}) copy-start(bf16[32,256]{1,0:T(8,128)(2,1)} %param.21) | copy-start | bytes 49156
  51.0 11.3 %all-to-all-start.4 = ((f32[32,2,8]{2,1,0:T(2,128)}), f32[32,2,8]{2,1,0:T(2,128)S(1)}, u32[]{:S(2)}, u32[]{:S(2)}) async-start(f32[32,2,8]{2,1,0:T(2,128)} %reshape.213), calls=%async_computation.4 | async-start | bytes 65536 | tf_op jit(solution)/shard_map/all_to_all | solution.py:103
  62.2 12.3 %all-to-all-start.3 = ((f32[32,2,8]{2,1,0:T(2,128)}), f32[32,2,8]{2,1,0:T(2,128)S(1)}, u32[]{:S(2)}, u32[]{:S(2)}) async-start(f32[32,2,8]{2,1,0:T(2,128)} %reshape.206), calls=%async_computation.3 | async-start | bytes 65536 | tf_op jit(solution)/shard_map/all_to_all | solution.py:96
  69.8 19.1 %copy-start.5 = (f32[32,2,4,160]{3,2,1,0:T(4,128)S(1)}, f32[32,2,4,160]{3,2,1,0:T(4,128)}, u32[]{:S(2)}) copy-start(f32[32,2,4,160]{3,2,1,0:T(4,128)} %copy-done.4) | copy-start | bytes 491524
  74.6 13.3 %all-to-all-start.2 = ((f32[32,2,1024]{2,1,0:T(2,128)}), f32[32,2,1024]{2,1,0:T(2,128)S(1)}, u32[]{:S(2)}, u32[]{:S(2)}) async-start(f32[32,2,1024]{2,1,0:T(2,128)} %reshape.204), calls=%async_computation.2 | async-start | bytes 524288 | tf_op jit(solution)/shard_map/all_to_all | solution.py:89
  78.9 62.2 %all-reduce.2.cloned.1.call-start = ((), (), s32[]{:S(2)}) async-start(), calls=%async_computation.7 | async-start | bytes 1310720 | tf_op jit(solution)/shard_map/psum | solution.py:161
  91.5 49.6 %copy-start.3 = (bf16[32,5120]{1,0:T(8,128)(2,1)S(1)}, bf16[32,5120]{1,0:T(8,128)(2,1)}, u32[]{:S(2)}) copy-start(bf16[32,5120]{1,0:T(8,128)(2,1)} %param.18) | copy-start | bytes 983044
  91.5 50.9 %copy-start.7 = (f32[5120]{0:T(1024)S(1)}, f32[5120]{0:T(1024)}, u32[]{:S(2)}) copy-start(f32[5120]{0:T(1024)} %param.30) | copy-start | bytes 61444
  98.4 103.4 %all-gather.2.cloned.1.call-start = ((), (), s32[]{:S(2)}) async-start(), calls=%async_computation.8 | async-start | bytes 10813440 | tf_op jit(solution)/shard_map/all_gather | solution.py:164
  143.4 759.3 %reduce-scatter.2.cloned.1.call-start = ((), (), s32[]{:S(2)}) async-start(), calls=%async_computation.9 | async-start | bytes 21135360 | tf_op jit(solution)/shard_map/reduce_scatter | solution.py:179
  228.8 675.5 %copy-start.1 = (bf16[5120,256]{1,0:T(8,128)(2,1)S(1)}, bf16[5120,256]{1,0:T(8,128)(2,1)}, u32[]{:S(2)}) copy-start(bf16[5120,256]{1,0:T(8,128)(2,1)} %param.32) | copy-start | bytes 7864324
Sparse Core Ops, SparseCore 0:
  98.5 42.6 all-reduce.1
  143.5 58.2 all-gather.1
  229.0 673.7 reduce-scatter.1
where the time goes:
time: 912 us; the launch traced here: 911 us
  waiting for transfers between devices  753 us (83%)
  matrix products  45.3 us (5%)
  blocking collectives  35 us (4%)
  starting transfers between devices  28.4 us (3%)
  local copies, waits for them, and re-layouts  23.9 us (3%)
  between operations  13.4 us (1%)
  other arithmetic  12.3 us (1%)
    reduce_scatter x1, waiting for transfers between devices, shards(): lax.psum_scatter(jnp.dot(hidden, down_rows, preferred_element_type=jnp.fl...  674 us
    psum x1, waiting for transfers between devices, shards(): summed = lax.psum(projected, 'head')  42.6 us
    all_to_all x1, blocking collectives, shards(): lax.all_to_all(down_proj, 'head', split_axis=0, concat_axis=1, tiled=True)  35 us
    all_gather x1, waiting for transfers between devices, shards(): lax.all_gather((resid_f * lax.rsqrt(jnp.mean(resid_f * resid_f, axis=-1,...  19 us
    dot_general x1, matrix products, shards(): jnp.dot(hidden, down_rows, preferred_element_type=jnp.float32)  18.4 us
  transfers between devices with their start and end apart: 8, of which 7 were waited for; matrix products, arithmetic and copies ran while one was open for 3% of the time, Pallas kernels for 0%

commit v1 on v0

--- a/solution.py
+++ b/solution.py
@@ -49,31 +49,40 @@
     order_in = jnp.sum(before * holder_hot, axis=1)
     slot_of = holder * slot_cap + order_in
     placing = slot_of[:, None] == jnp.arange(slot_total)[None, :]
-    send_query = (
-        jnp.einsum(
-            "rs,rc->sc", placing.astype(jnp.bfloat16), query, preferred_element_type=jnp.float32
-        )
-        .astype(jnp.bfloat16)
-        .reshape(n_req, slot_cap, col_width)
-    )
-    send_group = (
-        jnp.sum(placing.astype(jnp.int32) * (local_group[:, None] + 1), axis=0) - 1
-    ).reshape(n_req, slot_cap)
+    sent_rows = jnp.einsum(
+        "rs,rc->sc",
+        placing.astype(jnp.bfloat16),
+        jnp.concatenate(
+            [
+                query,
+                jnp.broadcast_to(
+                    (local_group[:, None] + 1).astype(jnp.bfloat16), (row_count, HEAD_WIDTH)
+                ),
+            ],
+            axis=1,
+        ),
+        preferred_element_type=jnp.float32,
+    ).astype(jnp.bfloat16)
     keys_all = group_prompt_keys.reshape(group_count * prompt_size, kv_local, HEAD_WIDTH)
     values_all = group_prompt_values.reshape(group_count * prompt_size, kv_local, HEAD_WIDTH)
     key_group = jnp.arange(group_count * prompt_size) // prompt_size
     key_live = jnp.arange(group_count * prompt_size) % prompt_size < jnp.repeat(
         prompt_len, prompt_size
     )
-    recv_query = lax.all_to_all(send_query, "req", split_axis=0, concat_axis=0, tiled=True)
-    recv_group = lax.all_to_all(send_group, "req", split_axis=0, concat_axis=0, tiled=True)
-    sources, item_count = recv_group.shape
-    flat_query = recv_query.reshape(sources * item_count, kv_local, each_key_value, HEAD_WIDTH)
+    recv = lax.all_to_all(
+        sent_rows.reshape(n_req, slot_cap, col_width + HEAD_WIDTH),
+        "req",
+        split_axis=0,
+        concat_axis=0,
+        tiled=True,
+    ).reshape(slot_total, col_width + HEAD_WIDTH)
+    recv_group = recv[:, col_width].astype(jnp.int32) - 1
+    flat_query = recv[:, :col_width].reshape(slot_total, kv_local, each_key_value, HEAD_WIDTH)
     scores = (
         jnp.einsum("nkrd,pkd->nkrp", flat_query, keys_all, preferred_element_type=jnp.float32)
         * scale_of_scores
     )
-    usable = (recv_group.reshape(sources * item_count)[:, None] == key_group[None, :]) & key_live[
+    usable = (recv_group[:, None] == key_group[None, :]) & key_live[
         None, :
     ]
     masked = jnp.where(usable[:, None, None, :], scores, MASKED_SCORE)
@@ -86,34 +95,27 @@
         values_all,
         preferred_element_type=jnp.float32,
     )
-    back_mix = lax.all_to_all(
-        mixture.reshape(sources, item_count, col_width),
+    back = lax.all_to_all(
+        jnp.concatenate(
+            [
+                mixture.reshape(slot_total, col_width),
+                largest.reshape(slot_total, head_local),
+                totals.reshape(slot_total, head_local),
+                jnp.zeros((slot_total, HEAD_WIDTH - 2 * head_local), jnp.float32),
+            ],
+            axis=1,
+        ).reshape(n_req, slot_cap, col_width + HEAD_WIDTH),
         "req",
         split_axis=0,
         concat_axis=0,
         tiled=True,
     )
-    back_peak = lax.all_to_all(
-        largest.reshape(sources, item_count, head_local),
-        "req",
-        split_axis=0,
-        concat_axis=0,
-        tiled=True,
-    )
-    back_total = lax.all_to_all(
-        totals.reshape(sources, item_count, head_local),
-        "req",
-        split_axis=0,
-        concat_axis=0,
-        tiled=True,
-    )
-    shared_mix = jnp.take(back_mix.reshape(slot_total, col_width), slot_of, axis=0).reshape(
-        row_count, kv_local, each_key_value, HEAD_WIDTH
-    )
-    shared_max = jnp.take(back_peak.reshape(slot_total, head_local), slot_of, axis=0).reshape(
+    shared = jnp.take(back.reshape(slot_total, col_width + HEAD_WIDTH), slot_of, axis=0)
+    shared_mix = shared[:, :col_width].reshape(row_count, kv_local, each_key_value, HEAD_WIDTH)
+    shared_max = shared[:, col_width : col_width + head_local].reshape(
         row_count, kv_local, each_key_value
     )
-    shared_total = jnp.take(back_total.reshape(slot_total, head_local), slot_of, axis=0).reshape(
+    shared_total = shared[:, col_width + head_local : col_width + 2 * head_local].reshape(
         row_count, kv_local, each_key_value
     )
     query_rows = query.reshape(row_count, kv_local, each_key_value, HEAD_WIDTH)
@@ -158,8 +160,11 @@
     projected = jnp.dot(attention, out_proj, preferred_element_type=jnp.float32)
     sub_rows = row_count // n_head
     head_index = lax.axis_index("head")
-    summed = lax.psum(projected, "head")
-    residual = (hidden_in.astype(jnp.float32) + summed).astype(jnp.bfloat16)
+    parts = lax.all_to_all(
+        projected.reshape(n_head, sub_rows, -1), "head", split_axis=0, concat_axis=0, tiled=True
+    )
+    own_in = lax.dynamic_slice_in_dim(hidden_in, head_index * sub_rows, sub_rows, 0)
+    residual = (own_in.astype(jnp.float32) + jnp.sum(parts, axis=0)).astype(jnp.bfloat16)
     resid_f = residual.astype(jnp.float32)
     segment = lax.all_gather(
         (
@@ -167,22 +172,23 @@
             * lax.rsqrt(jnp.mean(resid_f * resid_f, axis=-1, keepdims=True) + 1e-05)
             * norm_gain
         ).astype(jnp.bfloat16),
-        "req",
+        ("req", "head"),
         axis=0,
         tiled=True,
     )
     gate_vals = jnp.dot(segment, gate_proj, preferred_element_type=jnp.float32)
     up_vals = jnp.dot(segment, up_proj, preferred_element_type=jnp.float32)
     hidden = (jax.nn.silu(gate_vals) * up_vals).astype(jnp.bfloat16)
-    own_rows = lax.dynamic_slice_in_dim(residual, head_index * sub_rows, sub_rows, 0)
-    down_rows = lax.all_to_all(down_proj, "head", split_axis=0, concat_axis=1, tiled=True)
+    hidden_all = lax.all_gather(hidden, "head", axis=0)
+    down_parts = down_proj.reshape(n_head, hidden.shape[1], -1)
     lowered = lax.psum_scatter(
-        jnp.dot(hidden, down_rows, preferred_element_type=jnp.float32),
-        ("req", "head"),
+        jnp.einsum("hru,huc->rc", hidden_all, down_parts, preferred_element_type=jnp.float32),
+        "req",
         scatter_dimension=0,
         tiled=True,
     )
-    return (own_rows.astype(jnp.float32) + lowered).astype(jnp.bfloat16)
+    lowered = lax.all_to_all(lowered, "head", split_axis=0, concat_axis=1, tiled=True)
+    return (resid_f + lowered).astype(jnp.bfloat16)
 
 
 def solution(mesh):

time: 912 us -> 328 us (0.36)
  waiting for transfers between devices: 753 us -> 201 us
  blocking collectives: 35 us -> 10.5 us
    reduce_scatter x1, waiting for transfers between devices: 674 us -> 84.6 us  [shards(): lax.psum_scatter(jnp.einsum('hru,huc->rc', hidden_all, down_parts, prefer...]
    all_gather x1, waiting for transfers between devices: 19 us -> 67.5 us  [shards(): lax.all_gather((resid_f * lax.rsqrt(jnp.mean(resid_f * resid_f, axis=-1,...]
    psum x1 -> x0, waiting for transfers between devices: 42.6 us -> none  [shards(): summed = lax.psum(projected, 'head')]
    all_gather x0 -> x1, waiting for transfers between devices: none -> 29.3 us  [shards(): hidden_all = lax.all_gather(hidden, 'head', axis=0)]
    all_to_all x1, blocking collectives: 35 us -> 10.5 us  [shards(): lax.all_to_all(lowered, 'head', split_axis=0, concat_axis=1, tiled=True)]
    all_to_all x5 -> x3, starting transfers between devices: 28.1 us -> 20.1 us  [the longest x1 7.4 us: shards(): lax.all_to_all(sent_rows.reshape(n_req, slot_cap, col_width + HEAD_WIDTH)...]
    dot_general x2 -> x3, matrix products: 19.6 us -> 11.6 us  [the longest x1 6.77 us: shards(): jnp.einsum('hru,huc->rc', hidden_all, down_parts, preferred_element_type=...]
    all_to_all x5 -> x3, waiting for transfers between devices: 17 us -> 19.8 us  [the longest x1 11.3 us: shards(): lax.all_to_all(projected.reshape(n_head, sub_rows, -1), 'head', split_axi...]
  transfers between devices with their start and end apart: 8 -> 6, of which waited for: 7 -> 5; matrix products, arithmetic and copies ran while one was open for 3% -> 9% of each run, Pallas kernels for 0% -> 0%
where the time goes in v1:
time: 328 us; the launch traced here: 326 us
  waiting for transfers between devices  201 us (61%)
  matrix products  37.8 us (12%)
  local copies, waits for them, and re-layouts  27 us (8%)
  starting transfers between devices  20.4 us (6%)
  other arithmetic  16.1 us (5%)
  between operations  13.3 us (4%)
  blocking collectives  10.5 us (3%)
    reduce_scatter x1, waiting for transfers between devices, shards(): lax.psum_scatter(jnp.einsum('hru,huc->rc', hidden_all, down_parts, prefer...  84.6 us
    all_gather x1, waiting for transfers between devices, shards(): lax.all_gather((resid_f * lax.rsqrt(jnp.mean(resid_f * resid_f, axis=-1,...  67.5 us
    all_gather x1, waiting for transfers between devices, shards(): hidden_all = lax.all_gather(hidden, 'head', axis=0)  29.3 us
    all_to_all x1, waiting for transfers between devices, shards(): lax.all_to_all(projected.reshape(n_head, sub_rows, -1), 'head', split_axi...  11.3 us
    all_to_all x1, blocking collectives, shards(): lax.all_to_all(lowered, 'head', split_axis=0, concat_axis=1, tiled=True)  10.5 us
    all_to_all x1, waiting for transfers between devices, shards(): lax.all_to_all(jnp.concatenate([mixture.reshape(slot_total, col_width), l...  8.56 us
    all_to_all x1, starting transfers between devices, shards(): lax.all_to_all(sent_rows.reshape(n_req, slot_cap, col_width + HEAD_WIDTH)...  7.4 us
    all_to_all x1, starting transfers between devices, shards(): lax.all_to_all(jnp.concatenate([mixture.reshape(slot_total, col_width), l...  7.38 us
  transfers between devices with their start and end apart: 6, of which 5 were waited for; matrix products, arithmetic and copies ran while one was open for 9% of the time, Pallas kernels for 0%

profile of v1, /device:TPU:0, one launch (start us, length us, event | category | flops | bytes accessed | tf_op | source)
XLA Modules:
  0.0 326.4 jit_solution(3456983496252065622)
XLA Ops:
  10.7 7.4 %all-to-all-start = ((bf16[32,2,1152]{2,1,0:T(2,128)(2,1)}), bf16[32,2,1152]{2,1,0:T(2,128)(2,1)S(1)}, u32[]{:S(2)}, u32[]{:S(2)}) async-start(bf16[32,2,1152]{2,1,0:T(2,128)(2,1)} %reshape.177), calls=%async_computation | async-start | bytes 294912 | tf_op jit(solution)/shard_map/all_to_all | solution.py:72
  18.1 1.5 reshape.186
  19.6 1.3 broadcast_in_dim.44
  20.9 1.3 reshape.179
  23.5 1.3 iota_compare_fusion
  24.8 1.3 reshape.210
  26.1 1.7 fusion.75
  27.8 1.4 copy.84
  29.2 4.5 %fusion.74 = (f32[32,2,4]{2,1,0:T(2,128)}, f32[32,2,4,160]{3,2,1,0:T(4,128)}) fusion(bf16[32,2,4,128]{3,2,1,0:T(4,128)(2,1)} %reshape.186, pred[32,160]{1,0:T(8,128)(4,1)} %iota_compare_fusion, bf16[32,160,256]{2,1,0:T(8,128)(2,1)} %param.20), kind=kOutput, calls=%fused_computation.87 | convolution fusion | flops 10608384 | bytes 2856960 | tf_op jit(solution)/shard_map/bkrd,btkd->bkrt/dot_general | solution.py:125
  33.7 1.4 copy.72
  36.5 1.4 copy.74
  37.8 1.8 fusion.42
  39.7 1.3 reshape.192
  41.0 1.4 copy.76
  42.4 1.4 copy.79
  44.9 2.0 reshape.182
  49.0 1.6 slice.23
  52.4 3.5 %fusion.73 = (f32[64,2,4]{0,2,1:T(4,128)S(1)}, f32[64,2,4,1536]{3,0,2,1:T(8,128)}) fusion(bf16[1536,2,128,1]{2,1,0,3:T(2,128)(2,1)} %bitcast.72, bf16[64,2,4,128]{3,2,1,0:T(4,128)(2,1)S(1)} %reshape.180, pred[64,1536]{1,0:T(8,128)(4,1)S(1)} %compare_and_fusion), kind=kOutput, calls=%fused_computation.86 | convolution fusion | flops 203685376 | bytes 4163584 | tf_op jit(solution)/shard_map/nkrd,pkd->nkrp/dot_general | solution.py:82
  56.0 2.6 fusion.4
  61.5 7.4 %all-to-all-start.1 = ((f32[32,2,1152]{2,1,0:T(2,128)}), f32[32,2,1152]{2,1,0:T(2,128)S(1)}, u32[]{:S(2)}, u32[]{:S(2)}) async-start(f32[32,2,1152]{2,1,0:T(2,128)} %concatenate.17), calls=%async_computation.1 | async-start | bytes 589824 | tf_op jit(solution)/shard_map/all_to_all | solution.py:98
  69.5 8.6 %all-to-all-done.1 = f32[32,2,1152]{2,1,0:T(2,128)S(1)} async-done(((f32[32,2,1152]{2,1,0:T(2,128)}), f32[32,2,1152]{2,1,0:T(2,128)S(1)}, u32[]{:S(2)}, u32[]{:S(2)}) %all-to-all-start.1) | async-done | bytes 294944 | tf_op jit(solution)/shard_map/all_to_all | solution.py:98
  80.3 2.6 fusion.37
  82.9 6.7 %fusion = f32[4,8,5120]{2,1,0:T(8,128)} fusion(bf16[4,8,1024]{2,1,0:T(8,128)(2,1)S(1)} %convert_element_type.74, bf16[1024,5120]{1,0:T(8,128)(2,1)} %param.27), kind=kOutput, calls=%fused_computation.1 | convolution fusion | flops 335544320 | bytes 11206656 | tf_op jit(solution)/shard_map/dot_general | solution.py:160
  89.6 5.3 %all-to-all-start.2 = ((f32[4,8,5120]{2,1,0:T(8,128)}), f32[4,8,5120]{2,1,0:T(8,128)S(1)}, u32[]{:S(2)}, u32[]{:S(2)}) async-start(f32[4,8,5120]{2,1,0:T(8,128)} %fusion), calls=%async_computation.2 | async-start | bytes 1310720 | tf_op jit(solution)/shard_map/all_to_all | solution.py:163
  94.9 11.3 %all-to-all-done.2 = f32[4,8,5120]{2,1,0:T(8,128)S(1)} async-done(((f32[4,8,5120]{2,1,0:T(8,128)}), f32[4,8,5120]{2,1,0:T(8,128)S(1)}, u32[]{:S(2)}, u32[]{:S(2)}) %all-to-all-start.2) | async-done | bytes 655392 | tf_op jit(solution)/shard_map/all_to_all | solution.py:163
  108.3 67.5 %all-gather.4.cloned.1.call-done = bf16[1024,5120]{1,0:T(8,128)(2,1)} async-done(((bf16[8,5120]{1,0:T(8,128)(2,1)}), bf16[1024,5120]{1,0:T(8,128)(2,1)}) %all-gather.4.cloned.1.call-update) | async-done | bytes 10485776 | tf_op jit(solution)/shard_map/all_gather | solution.py:169
  175.7 6.6 %fusion.76 = f32[1024,256]{1,0:T(8,128)S(1)} fusion(bf16[1024,5120]{1,0:T(8,128)(2,1)} %all-gather.4.cloned.1.call-done, bf16[5120,256]{1,0:T(8,128)(2,1)} %param.29), kind=kOutput, calls=%fused_computation.89 | convolution fusion | flops 2684354560 | bytes 14155776 | tf_op jit(solution)/shard_map/dot_general | solution.py:179
  184.2 3.7 %fusion.15 = bf16[1024,256]{1,0:T(8,128)(2,1)} fusion(bf16[1024,5120]{1,0:T(8,128)(2,1)S(1)} %copy-done.9, bf16[5120,256]{1,0:T(8,128)(2,1)S(1)} %copy-done.10, f32[1024,256]{1,0:T(8,128)S(1)} %fusion.76), kind=kOutput, calls=%fused_computation.20 | convolution fusion | flops 2685927424 | bytes 14680064 | tf_op jit(solution)/shard_map/dot_general | solution.py:180
  188.0 29.3 %all-gather.6.cloned.1.call-done = bf16[4096,256]{1,0:T(8,128)(2,1)} async-done(((bf16[1024,256]{1,0:T(8,128)(2,1)}), bf16[4096,256]{1,0:T(8,128)(2,1)}) %all-gather.6.cloned.1.call-update) | async-done | bytes 2097168 | tf_op jit(solution)/shard_map/all_gather | solution.py:182
  217.3 6.8 %convolution_bitcast_fusion = f32[1024,1280]{1,0:T(8,128)} fusion(bf16[4,1024,256]{2,1,0:T(8,128)(2,1)} %bitcast.77, bf16[4,256,1280]{2,1,0:T(8,128)(2,1)S(1)} %bitcast.70), kind=kOutput, calls=%fused_computation.3 | convolution fusion | flops 2684354560 | bytes 9961472 | tf_op jit(solution)/shard_map/hru,huc->rc/dot_general | solution.py:185
  224.1 84.6 %reduce-scatter.2.cloned.1.call-done = f32[32,1280]{1,0:T(8,128)} async-done(((f32[1024,1280]{1,0:T(8,128)}), f32[32,1280]{1,0:T(8,128)}) %reduce-scatter.2.cloned.1.call-update) | async-done | bytes 163856 | tf_op jit(solution)/shard_map/reduce_scatter | solution.py:184
  308.6 10.5 %all_to_all.34 = f32[4,8,1280]{2,1,0:T(8,128)S(1)} all-to-all(f32[4,8,1280]{2,1,0:T(8,128)} %bitcast.74), channel_id=1, replica_groups=mesh['req'=32,'head'=4] {'head'}, dimensions={0} | all-to-all | bytes 327680 | tf_op jit(solution)/shard_map/all_to_all | solution.py:190
  (74 shorter events, 22.1 us)
Async XLA Ops:
  6.5 210.7 %copy-start = (bf16[1024,1280]{1,0:T(8,128)(2,1)S(1)}, bf16[1024,1280]{1,0:T(8,128)(2,1)}, u32[]{:S(2)}) copy-start(bf16[1024,1280]{1,0:T(8,128)(2,1)} %param.31) | copy-start | bytes 7864324
  6.5 37.3 %copy-start.2 = (bf16[3,512,256]{2,1,0:T(8,128)(2,1)S(1)}, bf16[3,512,256]{2,1,0:T(8,128)(2,1)}, u32[]{:S(2)}) copy-start(bf16[3,512,256]{2,1,0:T(8,128)(2,1)} %param.22) | copy-start | bytes 2359300
  8.2 0.6 copy-start.8
  10.7 36.8 %all-to-all-start = ((bf16[32,2,1152]{2,1,0:T(2,128)(2,1)}), bf16[32,2,1152]{2,1,0:T(2,128)(2,1)S(1)}, u32[]{:S(2)}, u32[]{:S(2)}) async-start(bf16[32,2,1152]{2,1,0:T(2,128)(2,1)} %reshape.177), calls=%async_computation | async-start | bytes 294912 | tf_op jit(solution)/shard_map/all_to_all | solution.py:72
  56.0 2.8 copy-start.1
  59.6 20.3 %copy-start.4 = (f32[32,2,1,4]{0,3,1,2:T(4,128)S(1)}, f32[32,2,1,4]{0,3,1,2:T(4,128)}, u32[]{:S(2)}) copy-start(f32[32,2,1,4]{0,3,1,2:T(4,128)} %copy.84) | copy-start | bytes 3076
  59.6 20.3 %copy-start.5 = (f32[32,2,4]{0,2,1:T(4,128)S(1)}, f32[32,2,4]{0,2,1:T(4,128)}, u32[]{:S(2)}) copy-start(f32[32,2,4]{0,2,1:T(4,128)} %get-tuple-element.8) | copy-start | bytes 3076
  59.6 20.3 %copy-start.7 = (f32[32,2,4]{0,2,1:T(4,128)S(1)}, f32[32,2,4]{0,2,1:T(4,128)}, u32[]{:S(2)}) copy-start(f32[32,2,4]{0,2,1:T(4,128)} %copy.79) | copy-start | bytes 3076
  59.8 20.5 %copy-start.3 = (f32[32,2,4,160]{3,2,1,0:T(4,128)S(1)}, f32[32,2,4,160]{3,2,1,0:T(4,128)}, u32[]{:S(2)}) copy-start(f32[32,2,4,160]{3,2,1,0:T(4,128)} %get-tuple-element.21) | copy-start | bytes 491524
  61.5 16.6 %all-to-all-start.1 = ((f32[32,2,1152]{2,1,0:T(2,128)}), f32[32,2,1152]{2,1,0:T(2,128)S(1)}, u32[]{:S(2)}, u32[]{:S(2)}) async-start(f32[32,2,1152]{2,1,0:T(2,128)} %concatenate.17), calls=%async_computation.1 | async-start | bytes 589824 | tf_op jit(solution)/shard_map/all_to_all | solution.py:98
  82.9 24.4 %copy-start.6 = (f32[5120]{0:T(1024)S(1)}, f32[5120]{0:T(1024)}, u32[]{:S(2)}) copy-start(f32[5120]{0:T(1024)} %param.28) | copy-start | bytes 61444
  89.6 16.6 %all-to-all-start.2 = ((f32[4,8,5120]{2,1,0:T(8,128)}), f32[4,8,5120]{2,1,0:T(8,128)S(1)}, u32[]{:S(2)}, u32[]{:S(2)}) async-start(f32[4,8,5120]{2,1,0:T(8,128)} %fusion), calls=%async_computation.2 | async-start | bytes 1310720 | tf_op jit(solution)/shard_map/all_to_all | solution.py:163
  94.9 80.8 %all-gather.4.cloned.1.call-start = ((), (), s32[]{:S(2)}) async-start(), calls=%async_computation.5 | async-start | bytes 10567680 | tf_op jit(solution)/shard_map/all_gather | solution.py:169
  108.0 109.2 %all-gather.6.cloned.1.call-start = ((), (), s32[]{:S(2)}) async-start(), calls=%async_computation.7 | async-start | bytes 2621440 | tf_op jit(solution)/shard_map/all_gather | solution.py:182
  175.7 7.8 %copy-start.9 = (bf16[1024,5120]{1,0:T(8,128)(2,1)S(1)}, bf16[1024,5120]{1,0:T(8,128)(2,1)}, u32[]{:S(2)}) copy-start(bf16[1024,5120]{1,0:T(8,128)(2,1)} %all-gather.4.cloned.1.call-done) | copy-start | bytes 31457284
  175.7 8.5 %copy-start.10 = (bf16[5120,256]{1,0:T(8,128)(2,1)S(1)}, bf16[5120,256]{1,0:T(8,128)(2,1)}, u32[]{:S(2)}) copy-start(bf16[5120,256]{1,0:T(8,128)(2,1)} %param.30) | copy-start | bytes 7864324
  187.9 120.7 %reduce-scatter.2.cloned.1.call-start = ((), (), s32[]{:S(2)}) async-start(), calls=%async_computation.6 | async-start | bytes 5406720 | tf_op jit(solution)/shard_map/reduce_scatter | solution.py:184
Sparse Core Ops, SparseCore 0:
  108.2 67.5 all-gather.3
  188.1 29.1 all-gather.5
  224.2 84.3 reduce-scatter.1

commit v2 on v1

--- a/solution.py
+++ b/solution.py
@@ -1,7 +1,11 @@
+import functools
+
 import jax
 import jax.numpy as jnp
 from jax import lax
-from jax.sharding import PartitionSpec as P
+from jax.experimental import pallas as pl
+from jax.experimental.pallas import tpu as pltpu
+from jax.sharding import Mesh, PartitionSpec as P
 
 QUERY_HEADS = 32
 KEY_VALUE_HEADS = 8
@@ -9,6 +13,107 @@
 
 
 MASKED_SCORE = -1e30
+
+
+REQ = ("y", "x", "core")
+RING = 4
+PIECE = 64
+K_BLOCK = 512
+
+
+def shift(value, axis, step):
+    size = lax.axis_size(axis)
+    return lax.ppermute(value, axis, [(i, (i + step) % size) for i in range(size)])
+
+
+def ring_pieces(value, axis):
+    return [value] + [shift(value, axis, step) for step in (1, 2, 3)]
+
+
+def mlp_in_kernel(*refs, n):
+    rows, (gate_a, gate_b, up_a, up_b, out, acc) = refs[:n], refs[n:]
+    step = pl.program_id(0)
+    block = jnp.concatenate([r[...] for r in rows], axis=0)
+    width = gate_a.shape[1]
+    for i, w in enumerate((gate_a, gate_b, up_a, up_b)):
+        part = jnp.dot(block, w[...], preferred_element_type=jnp.float32)
+        cols = pl.ds(i * width, width)
+
+        @pl.when(step == 0)
+        def _():
+            acc[:, cols] = part
+
+        @pl.when(step > 0)
+        def _():
+            acc[:, cols] += part
+
+    @pl.when(step == pl.num_programs(0) - 1)
+    def _():
+        gate = acc[:, : 2 * width]
+        out[...] = (gate / (1.0 + jnp.exp(-gate)) * acc[:, 2 * width :]).astype(out.dtype)
+
+
+def mlp_in(pieces, weights):
+    n = len(pieces)
+    depth, width = weights[0].shape
+    rows = sum(p.shape[0] for p in pieces)
+    return pl.pallas_call(
+        functools.partial(mlp_in_kernel, n=n),
+        grid=(depth // K_BLOCK,),
+        in_specs=[pl.BlockSpec((p.shape[0], K_BLOCK), lambda k: (0, k)) for p in pieces]
+        + [pl.BlockSpec((K_BLOCK, width), lambda k: (k, 0))] * 4,
+        out_specs=pl.BlockSpec((rows, 2 * width), lambda k: (0, 0)),
+        out_shape=jax.ShapeDtypeStruct((rows, 2 * width), jnp.bfloat16),
+        scratch_shapes=[pltpu.VMEM((rows, 4 * width), jnp.float32)],
+        name="mlp_in",
+    )(*pieces, *weights)
+
+
+def mlp_out_kernel(index, *refs, groups):
+    hidden, (down_a, down_b, out, acc) = refs[: RING * len(groups)], refs[RING * len(groups) :]
+    step = pl.program_id(0)
+    half = down_a.shape[0]
+    for i in range(RING):
+
+        @pl.when(step == i)
+        def _():
+            block = jnp.concatenate([hidden[g * RING + i][...] for g in range(len(groups))], axis=0)
+            part = jnp.dot(
+                block[:, :half], down_a[...], preferred_element_type=jnp.float32
+            ) + jnp.dot(block[:, half:], down_b[...], preferred_element_type=jnp.float32)
+            acc[...] = part if i == 0 else acc[...] + part
+
+    @pl.when(step == RING - 1)
+    def _():
+        at = 0
+        for color, outer in [p for g in groups for p in g]:
+            for inner in range(RING):
+                place = index[RING + color * RING * RING + outer * RING + inner]
+                rows = PIECE // RING
+                out[pl.ds(place, 1), color * rows : (color + 1) * rows, :] = acc[
+                    at : at + rows, :
+                ].astype(out.dtype)[None]
+                at += rows
+
+
+def mlp_out(index, hidden, down_a, down_b, groups):
+    width = down_a.shape[1]
+    depth = down_a.shape[0] // RING
+    total = sum(PIECE * len(g) for g in groups)
+    flat = [h for g in hidden for h in g]
+    return pl.pallas_call(
+        functools.partial(mlp_out_kernel, groups=groups),
+        grid_spec=pltpu.PrefetchScalarGridSpec(
+            num_scalar_prefetch=1,
+            grid=(RING,),
+            in_specs=[pl.BlockSpec(h.shape, lambda k, ix: (0, 0)) for h in flat]
+            + [pl.BlockSpec((depth, width), lambda k, ix: (ix[k], 0))] * 2,
+            out_specs=pl.BlockSpec((RING * RING, total // RING // RING, width), lambda k, ix: (0, 0, 0)),
+            scratch_shapes=[pltpu.VMEM((total, width), jnp.float32)],
+        ),
+        out_shape=jax.ShapeDtypeStruct((RING * RING, total // RING // RING, width), jnp.bfloat16),
+        name="mlp_out",
+    )(index, *flat, down_a, down_b)
 
 
 def shards(
@@ -29,7 +134,10 @@
     up_proj,
     down_proj,
 ):
-    n_req = lax.axis_size("req")
+    gate_other = shift(gate_proj, "core", 1)
+    up_other = shift(up_proj, "core", 1)
+    down_other = shift(down_proj, "core", 1)
+    n_req = lax.axis_size(REQ)
     n_head = lax.axis_size("head")
     row_count = query.shape[0]
     kv_local = incoming_key.shape[1] // HEAD_WIDTH
@@ -71,7 +179,7 @@
     )
     recv = lax.all_to_all(
         sent_rows.reshape(n_req, slot_cap, col_width + HEAD_WIDTH),
-        "req",
+        REQ,
         split_axis=0,
         concat_axis=0,
         tiled=True,
@@ -105,7 +213,7 @@
             ],
             axis=1,
         ).reshape(n_req, slot_cap, col_width + HEAD_WIDTH),
-        "req",
+        REQ,
         split_axis=0,
         concat_axis=0,
         tiled=True,
@@ -161,58 +269,80 @@
     sub_rows = row_count // n_head
     head_index = lax.axis_index("head")
     parts = lax.all_to_all(
-        projected.reshape(n_head, sub_rows, -1), "head", split_axis=0, concat_axis=0, tiled=True
+        projected.astype(jnp.bfloat16).reshape(n_head, sub_rows, -1),
+        "head",
+        split_axis=0,
+        concat_axis=0,
+        tiled=True,
     )
     own_in = lax.dynamic_slice_in_dim(hidden_in, head_index * sub_rows, sub_rows, 0)
-    residual = (own_in.astype(jnp.float32) + jnp.sum(parts, axis=0)).astype(jnp.bfloat16)
+    residual = (
+        own_in.astype(jnp.float32) + jnp.sum(parts.astype(jnp.float32), axis=0)
+    ).astype(jnp.bfloat16)
     resid_f = residual.astype(jnp.float32)
-    segment = lax.all_gather(
-        (
-            resid_f
-            * lax.rsqrt(jnp.mean(resid_f * resid_f, axis=-1, keepdims=True) + 1e-05)
-            * norm_gain
-        ).astype(jnp.bfloat16),
-        ("req", "head"),
-        axis=0,
+    normed = (
+        resid_f
+        * lax.rsqrt(jnp.mean(resid_f * resid_f, axis=-1, keepdims=True) + 1e-05)
+        * norm_gain
+    ).astype(jnp.bfloat16)
+    block = lax.all_gather(normed, "head", axis=0, tiled=True)
+    half = row_count // 2
+    first_a = jnp.concatenate(ring_pieces(block[:half], "x"), axis=0)
+    first_b = jnp.concatenate(ring_pieces(block[half:], "y"), axis=0)
+    pieces = (ring_pieces(first_a, "y"), ring_pieces(first_b, "x"))
+    groups = (((0, 0), (1, 0)), ((0, 1), (0, 3), (1, 1), (1, 3)), ((0, 2), (1, 2)))
+    hidden = [
+        ring_pieces(
+            mlp_in([pieces[c][d] for c, d in g], (gate_proj, gate_other, up_proj, up_other)), "head"
+        )
+        for g in groups
+    ]
+    steps = jnp.arange(RING, dtype=jnp.int32)
+    at_y = (lax.axis_index("y") - steps) % RING
+    at_x = (lax.axis_index("x") - steps) % RING
+    index = jnp.concatenate(
+        [
+            (head_index - steps) % RING,
+            (at_y[:, None] * RING + at_x[None, :]).reshape(-1),
+            (at_y[None, :] * RING + at_x[:, None]).reshape(-1),
+        ]
+    )
+    partial = mlp_out(index, hidden, down_proj, down_other, groups)
+    lowered = lax.all_to_all(
+        partial.reshape(RING * RING * n_head, sub_rows, -1),
+        ("y", "x", "head"),
+        split_axis=0,
+        concat_axis=0,
         tiled=True,
-    )
-    gate_vals = jnp.dot(segment, gate_proj, preferred_element_type=jnp.float32)
-    up_vals = jnp.dot(segment, up_proj, preferred_element_type=jnp.float32)
-    hidden = (jax.nn.silu(gate_vals) * up_vals).astype(jnp.bfloat16)
-    hidden_all = lax.all_gather(hidden, "head", axis=0)
-    down_parts = down_proj.reshape(n_head, hidden.shape[1], -1)
-    lowered = lax.psum_scatter(
-        jnp.einsum("hru,huc->rc", hidden_all, down_parts, preferred_element_type=jnp.float32),
-        "req",
-        scatter_dimension=0,
-        tiled=True,
-    )
-    lowered = lax.all_to_all(lowered, "head", split_axis=0, concat_axis=1, tiled=True)
+    ).reshape(RING * RING, n_head, sub_rows, -1)
+    lowered = jnp.sum(lowered.astype(jnp.float32), axis=0)
+    lowered = jnp.swapaxes(lowered, 0, 1).reshape(sub_rows, -1)
     return (resid_f + lowered).astype(jnp.bfloat16)
 
 
 def solution(mesh):
+    mesh = Mesh(mesh.devices.reshape(RING, RING, 2, mesh.devices.shape[1]), REQ + ("head",))
     return jax.shard_map(
         shards,
         mesh=mesh,
         in_specs=(
-            P("req", None),
-            P("req", "head"),
-            P("req", "head"),
-            P("req", "head"),
-            P("req", None, "head"),
-            P("req", None, "head"),
-            P("req", None, "head"),
-            P("req", None, "head"),
-            P("req"),
-            P("req"),
-            P("req"),
+            P(REQ, None),
+            P(REQ, "head"),
+            P(REQ, "head"),
+            P(REQ, "head"),
+            P(REQ, None, "head"),
+            P(REQ, None, "head"),
+            P(REQ, None, "head"),
+            P(REQ, None, "head"),
+            P(REQ),
+            P(REQ),
+            P(REQ),
             P("head", None),
             P(),
-            P(None, ("req", "head")),
-            P(None, ("req", "head")),
-            P("req", "head"),
+            P(None, REQ + ("head",)),
+            P(None, REQ + ("head",)),
+            P(REQ, "head"),
         ),
-        out_specs=P(("req", "head"), None),
+        out_specs=P(REQ + ("head",), None),
         check_vma=False,
     )

time: 328 us -> 256 us (0.78)
  waiting for transfers between devices: 201 us -> 63.2 us
  Pallas kernels: 0 us -> 48.2 us
  starting transfers between devices: 20.4 us -> 45 us
  blocking collectives: 10.5 us -> 33.6 us
  matrix products: 37.8 us -> 19.9 us
  between operations: 13.3 us -> 0.34 us
    all_gather x2 -> x0, waiting for transfers between devices: 96.7 us -> none  [the longest x1 67.5 us: shards(): lax.all_gather((resid_f * lax.rsqrt(jnp.mean(resid_f * resid_f, axis=-1,...]
    reduce_scatter x1 -> x0, waiting for transfers between devices: 84.6 us -> none  [shards(): lax.psum_scatter(jnp.einsum('hru,huc->rc', hidden_all, down_parts, prefer...]
    pallas_call x0 -> x4, Pallas kernels: none -> 48.2 us  [the longest x3 40.5 us: mlp_in(): pl.pallas_call(functools.partial(mlp_in_kernel, n=n), grid=(depth // K_BL...]
    ppermute x0 -> x24, waiting for transfers between devices: none -> 47.4 us  [shift(): lax.ppermute(value, axis, [(i, (i + step) % size) for i in range(size)])]
    ppermute x0 -> x24, starting transfers between devices: none -> 25 us  [shift(): lax.ppermute(value, axis, [(i, (i + step) % size) for i in range(size)])]
    dot_general x3 -> x0, matrix products: 17.1 us -> none  [the longest x1 6.77 us: shards(): jnp.einsum('hru,huc->rc', hidden_all, down_parts, preferred_element_type=...]
    all_gather x0 -> x1, blocking collectives: none -> 12.6 us  [shards(): block = lax.all_gather(normed, 'head', axis=0, tiled=True)]
    all_to_all x1, blocking collectives: 10.5 us -> 21 us  [shards(): lax.all_to_all(partial.reshape(RING * RING * n_head, sub_rows, -1), ('y',...]
  transfers between devices with their start and end apart: 6 -> 27, of which waited for: 5 -> 12; matrix products, arithmetic and copies ran while one was open for 9% -> 13% of each run, Pallas kernels for 0% -> 16%
where the time goes in v2:
time: 256 us; the launch traced here: 254 us
  waiting for transfers between devices  63.2 us (25%)
  Pallas kernels  48.2 us (19%)
  starting transfers between devices  45 us (18%)
  blocking collectives  33.6 us (13%)
  local copies, waits for them, and re-layouts  26.6 us (10%)
  matrix products  19.9 us (8%)
  other arithmetic  17.3 us (7%)
    ppermute x24, waiting for transfers between devices, shift(): lax.ppermute(value, axis, [(i, (i + step) % size) for i in range(size)])  47.4 us
    pallas_call x3, Pallas kernels, mlp_in(): pl.pallas_call(functools.partial(mlp_in_kernel, n=n), grid=(depth // K_BL...  40.5 us
    ppermute x24, starting transfers between devices, shift(): lax.ppermute(value, axis, [(i, (i + step) % size) for i in range(size)])  25 us
    all_to_all x1, blocking collectives, shards(): lax.all_to_all(partial.reshape(RING * RING * n_head, sub_rows, -1), ('y',...  21 us
    all_gather x1, blocking collectives, shards(): block = lax.all_gather(normed, 'head', axis=0, tiled=True)  12.6 us
    all_to_all x1, waiting for transfers between devices, shards(): lax.all_to_all(jnp.concatenate([mixture.reshape(slot_total, col_width), l...  8.62 us
    pallas_call x1, Pallas kernels, mlp_out(): pl.pallas_call(functools.partial(mlp_out_kernel, groups=groups), grid_spe...  7.75 us
    all_to_all x1, starting transfers between devices, shards(): lax.all_to_all(sent_rows.reshape(n_req, slot_cap, col_width + HEAD_WIDTH)...  7.4 us
  transfers between devices with their start and end apart: 27, of which 12 were waited for; matrix products, arithmetic and copies ran while one was open for 13% of the time, Pallas kernels for 16%

profile of v2, /device:TPU:0, one launch (start us, length us, event | category | flops | bytes accessed | tf_op | source)
XLA Modules:
  0.0 254.2 jit_solution(6478902362828655469)
XLA Ops:
  4.1 7.4 %all-to-all-start = ((bf16[32,2,1152]{2,1,0:T(2,128)(2,1)}), bf16[32,2,1152]{2,1,0:T(2,128)(2,1)S(1)}, u32[]{:S(2)}, u32[]{:S(2)}) async-start(bf16[32,2,1152]{2,1,0:T(2,128)(2,1)} %reshape.252), calls=%async_computation | async-start | bytes 294912 | tf_op jit(solution)/shard_map/all_to_all | solution.py:180
  18.8 3.6 %fusion.77 = (f32[32,2,4]{2,1,0:T(2,128)}, f32[32,2,4,160]{3,2,1,0:T(4,128)}) fusion(bf16[32,2,4,128]{3,2,1,0:T(4,128)(2,1)} %reshape.261, pred[32,160]{1,0:T(8,128)(4,1)} %iota_compare_fusion, bf16[32,160,256]{2,1,0:T(8,128)(2,1)S(1)} %copy-done), kind=kOutput, calls=%fused_computation.105 | convolution fusion | flops 10608384 | bytes 2856960 | tf_op jit(solution)/shard_map/bkrd,btkd->bkrt/dot_general | solution.py:233
  30.4 1.8 fusion.40
  33.3 2.0 reshape.257
  45.0 3.5 %fusion.76 = (f32[64,2,4]{0,2,1:T(4,128)S(1)}, f32[64,2,4,1536]{3,0,2,1:T(8,128)}) fusion(bf16[1536,2,128,1]{2,1,0,3:T(2,128)(2,1)} %bitcast.65, bf16[64,2,4,128]{3,2,1,0:T(4,128)(2,1)S(1)} %reshape.255, pred[64,1536]{1,0:T(8,128)(4,1)S(1)} %compare_and_fusion), kind=kOutput, calls=%fused_computation.104 | convolution fusion | flops 203685376 | bytes 4163584 | tf_op jit(solution)/shard_map/nkrd,pkd->nkrp/dot_general | solution.py:190
  48.6 2.6 %fusion.3 = f32[64,2,4]{0,2,1:T(4,128)S(1)} fusion(f32[64,2,4,1536]{3,0,2,1:T(8,128)} %get-tuple-element.23, f32[64,2,4]{0,2,1:T(4,128)S(1)} %get-tuple-element.22), kind=kLoop, calls=%fused_computation.7 | loop fusion | flops 1572352 | bytes 3149824 | tf_op jit(solution)/shard_map/reduce_sum | solution.py:199
  54.0 7.4 %all-to-all-start.1 = ((f32[32,2,1152]{2,1,0:T(2,128)}), f32[32,2,1152]{2,1,0:T(2,128)S(1)}, u32[]{:S(2)}, u32[]{:S(2)}) async-start(f32[32,2,1152]{2,1,0:T(2,128)} %concatenate.26), calls=%async_computation.1 | async-start | bytes 589824 | tf_op jit(solution)/shard_map/all_to_all | solution.py:206
  62.0 8.6 %all-to-all-done.1 = f32[32,2,1152]{2,1,0:T(2,128)S(1)} async-done(((f32[32,2,1152]{2,1,0:T(2,128)}), f32[32,2,1152]{2,1,0:T(2,128)S(1)}, u32[]{:S(2)}, u32[]{:S(2)}) %all-to-all-start.1) | async-done | bytes 294944 | tf_op jit(solution)/shard_map/all_to_all | solution.py:206
  72.8 2.6 %fusion.35 = bf16[32,2,4,128]{3,2,1,0:T(4,128)(2,1)S(1)} fusion(f32[32,2,4,160]{3,2,1,0:T(4,128)S(1)} %copy-done.11, f32[32,2,4]{2,1,0:T(2,128)} %copy.74, f32[32,2,4,128]{3,2,1,0:T(4,128)S(1)} %reshape.259, f32[32,2,4]{2,1,0:T(2,128)S(1)} %copy.80, f32[32,2,4]{2,1,0:T(2,128)S(1)} %copy.77, f32[32,2,128]{2,1,0:T(2,128)} %reshape.269, ...), kind=kOutput, calls=%fused_computation.26 | convolution fusion | flops 10797056 | bytes 3019776 | tf_op jit(solution)/shard_map/bkrt,btkd->bkrd/dot_general | solution.py:254
  75.5 6.6 %fusion = bf16[4,8,5120]{2,1,0:T(8,128)(2,1)} fusion(bf16[32,1024]{1,0:T(8,128)(2,1)S(1)} %convert_element_type.82, bf16[1024,5120]{1,0:T(8,128)(2,1)} %param.27), kind=kOutput, calls=%fused_computation.2 | convolution fusion | flops 335708160 | bytes 10878976 | tf_op jit(solution)/shard_map/dot_general | solution.py:268
  82.1 5.3 %all-to-all-start.2 = ((bf16[4,8,5120]{2,1,0:T(8,128)(2,1)}), bf16[4,8,5120]{2,1,0:T(8,128)(2,1)S(1)}, u32[]{:S(2)}, u32[]{:S(2)}) async-start(bf16[4,8,5120]{2,1,0:T(8,128)(2,1)} %fusion), calls=%async_computation.2 | async-start | bytes 655360 | tf_op jit(solution)/shard_map/all_to_all | solution.py:271
  87.9 7.3 %all-to-all-done.2 = bf16[4,8,5120]{2,1,0:T(8,128)(2,1)S(1)} async-done(((bf16[4,8,5120]{2,1,0:T(8,128)(2,1)}), bf16[4,8,5120]{2,1,0:T(8,128)(2,1)S(1)}, u32[]{:S(2)}, u32[]{:S(2)}) %all-to-all-start.2) | async-done | bytes 327712 | tf_op jit(solution)/shard_map/all_to_all | solution.py:271
  97.0 12.6 %all_gather.3 = bf16[32,5120]{1,0:T(8,128)(2,1)S(1)} all-gather(bf16[8,5120]{1,0:T(8,128)(2,1)S(1)} %fusion.44), channel_id=1, replica_groups=mesh['y'=4,'x'=4,'core'=2,'head'=4] {'head'}, dimensions={0}, use_global_device_ids=true | all-gather | bytes 409600 | tf_op jit(solution)/shard_map/all_gather | solution.py:288
  112.6 2.4 collective-permute-done.2
  115.9 3.3 %collective-permute-done.1 = bf16[16,5120]{1,0:T(8,128)(2,1)S(1)} collective-permute-done((bf16[16,5120]{1,0:T(8,128)(2,1)S(1)}, bf16[16,5120]{1,0:T(8,128)(2,1)S(1)}, u32[]{:S(2)}, u32[]{:S(2)}) %collective-permute-start.1) | collective-permute-done | bytes 163872 | tf_op jit(solution)/shard_map/ppermute | solution.py:26
  123.0 2.4 collective-permute-done.5
  126.9 1.8 collective-permute-done.4
  129.0 4.7 %collective-permute-done.3 = bf16[16,5120]{1,0:T(8,128)(2,1)S(1)} collective-permute-done((bf16[16,5120]{1,0:T(8,128)(2,1)S(1)}, bf16[16,5120]{1,0:T(8,128)(2,1)S(1)}, u32[]{:S(2)}, u32[]{:S(2)}) %collective-permute-start.3) | collective-permute-done | bytes 163872 | tf_op jit(solution)/shard_map/ppermute | solution.py:26
  136.1 8.5 %collective-permute-done.11.refs_0_ = bf16[64,5120]{1,0:T(8,128)(2,1)S(1)} collective-permute-done((bf16[64,5120]{1,0:T(8,128)(2,1)S(1)}, bf16[64,5120]{1,0:T(8,128)(2,1)S(1)}, u32[]{:S(2)}, u32[]{:S(2)}) %collective-permute-start.11) | collective-permute-done | bytes 655392 | tf_op jit(solution)/shard_map/ppermute | solution.py:26
  144.7 3.2 %collective-permute-start.14 = (bf16[64,5120]{1,0:T(8,128)(2,1)}, bf16[64,5120]{1,0:T(8,128)(2,1)}, u32[]{:S(2)}, u32[]{:S(2)}) collective-permute-start(bf16[64,5120]{1,0:T(8,128)(2,1)} %pad_maximum_fusion.1.refs_1_), channel_id=1, source_target_pairs={{0,24},{8,0},{16,8},{24,16},{1,25},{9,1},{17,9},{25,17},{2,26},{10... | collective-permute-start | bytes 1966088 | tf_op jit(solution)/shard_map/ppermute | solution.py:26
  148.9 12.7 %mlp_in.3.refs_0_ = bf16[128,512]{1,0:T(8,128)(2,1)} custom-call(bf16[64,5120]{1,0:T(8,128)(2,1)} %copy-done.2, bf16[64,5120]{1,0:T(8,128)(2,1)} %pad_maximum_fusion.1.refs_1_, bf16[5120,256]{1,0:T(8,128)(2,1)} %refs_2_.3, bf16[5120,256]{1,0:T(8,128)(2,1)} %collective-permute-done.6.refs_3_.refs_5_, bf16[5120,256]{1,0:T(8,128)(2,1)} %refs_4_.5, ...), custom_call_target="tpu_custom_call" | custom-call | tf_op jit(solution)/shard_map/mlp_in/pallas_call | solution.py:60
  161.6 12.2 %collective-permute-done.13.refs_2_ = bf16[64,5120]{1,0:T(8,128)(2,1)} collective-permute-done((bf16[64,5120]{1,0:T(8,128)(2,1)}, bf16[64,5120]{1,0:T(8,128)(2,1)}, u32[]{:S(2)}, u32[]{:S(2)}) %collective-permute-start.13) | collective-permute-done | bytes 655392 | tf_op jit(solution)/shard_map/ppermute | solution.py:26
  173.9 2.2 collective-permute-start.9
  176.1 15.1 %mlp_in.4.refs_4_ = bf16[256,512]{1,0:T(8,128)(2,1)} custom-call(bf16[64,5120]{1,0:T(8,128)(2,1)} %copy-done.7, bf16[64,5120]{1,0:T(8,128)(2,1)} %copy-done.8, bf16[64,5120]{1,0:T(8,128)(2,1)} %collective-permute-done.13.refs_2_, bf16[64,5120]{1,0:T(8,128)(2,1)} %collective-permute-done.14.refs_3_, bf16[5120,256]{1,0:T(8,128)(2,1)} %refs_2_.3, ...), custom_call_target="tpu_custom_call" | custom-call | tf_op jit(solution)/shard_map/mlp_in/pallas_call | solution.py:60
  191.2 2.0 collective-permute-start.10
  193.3 12.7 %mlp_in.5.refs_8_ = bf16[128,512]{1,0:T(8,128)(2,1)} custom-call(bf16[64,5120]{1,0:T(8,128)(2,1)} %collective-permute-done.18.refs_0_, bf16[64,5120]{1,0:T(8,128)(2,1)} %collective-permute-done.19.refs_1_, bf16[5120,256]{1,0:T(8,128)(2,1)} %refs_2_.3, bf16[5120,256]{1,0:T(8,128)(2,1)} %collective-permute-done.6.refs_3_.refs_5_, bf16[5120,256]{1,0:T(8,128)(2,1)} %refs_4_.5, ...), custom_call_target="tpu_custom_call" | custom-call | tf_op jit(solution)/shard_map/mlp_in/pallas_call | solution.py:60
  206.0 2.0 collective-permute-start.16
  208.0 2.6 %collective-permute-start.17 = (bf16[256,512]{1,0:T(8,128)(2,1)S(1)}, bf16[256,512]{1,0:T(8,128)(2,1)}, u32[]{:S(2)}, u32[]{:S(2)}) collective-permute-start(bf16[256,512]{1,0:T(8,128)(2,1)S(1)} %copy-done.3), channel_id=1, source_target_pairs={{0,3},{1,0},{2,1},{3,2},{4,7},{5,4},{6,5},{7,6},{8,11},{9,8},{10,9... | collective-permute-start | bytes 786440 | tf_op jit(solution)/shard_map/ppermute | solution.py:26
  212.3 6.2 %collective-permute-done.20.refs_9_ = bf16[128,512]{1,0:T(8,128)(2,1)} collective-permute-done((bf16[128,512]{1,0:T(8,128)(2,1)}, bf16[128,512]{1,0:T(8,128)(2,1)}, u32[]{:S(2)}, u32[]{:S(2)}) %collective-permute-start.20) | collective-permute-done | bytes 131104 | tf_op jit(solution)/shard_map/ppermute | solution.py:26
  219.3 4.5 %collective-permute-done.22.refs_11_ = bf16[128,512]{1,0:T(8,128)(2,1)} collective-permute-done((bf16[128,512]{1,0:T(8,128)(2,1)}, bf16[128,512]{1,0:T(8,128)(2,1)}, u32[]{:S(2)}, u32[]{:S(2)}) %collective-permute-start.22) | collective-permute-done | bytes 131104 | tf_op jit(solution)/shard_map/ppermute | solution.py:26
  224.6 7.7 %mlp_out.1 = bf16[16,32,1280]{2,1,0:T(8,128)(2,1)} custom-call(s32[36]{0:T(128)} %pad_add_fusion.index, bf16[128,512]{1,0:T(8,128)(2,1)} %mlp_in.3.refs_0_, bf16[128,512]{1,0:T(8,128)(2,1)} %collective-permute-done.8.refs_1_, bf16[128,512]{1,0:T(8,128)(2,1)} %collective-permute-done.9.refs_2_, bf16[128,512]{1,0:T(8,128)(2,1)} %copy-done.12, ...), custom_call_target="tpu_custom_call" | custom-call | tf_op jit(solution)/shard_map/mlp_out/pallas_call | solution.py:104
  232.4 21.0 %all_to_all.20 = bf16[64,8,1280]{2,1,0:T(8,128)(2,1)S(1)} all-to-all(bf16[64,8,1280]{2,1,0:T(8,128)(2,1)} %bitcast.62), channel_id=1, replica_groups=mesh['y'=4,'x'=4,'core'=2,'head'=4] {'y','x','head'}, dimensions={0} | all-to-all | bytes 2621440 | tf_op jit(solution)/shard_map/all_to_all | solution.py:311
  (139 shorter events, 55.2 us)
Async XLA Ops:
  0.0 32.2 %copy-start.4 = (bf16[3,512,256]{2,1,0:T(8,128)(2,1)S(1)}, bf16[3,512,256]{2,1,0:T(8,128)(2,1)}, u32[]{:S(2)}) copy-start(bf16[3,512,256]{2,1,0:T(8,128)(2,1)} %param.22) | copy-start | bytes 2359300
  4.1 36.0 %all-to-all-start = ((bf16[32,2,1152]{2,1,0:T(2,128)(2,1)}), bf16[32,2,1152]{2,1,0:T(2,128)(2,1)S(1)}, u32[]{:S(2)}, u32[]{:S(2)}) async-start(bf16[32,2,1152]{2,1,0:T(2,128)(2,1)} %reshape.252), calls=%async_computation | async-start | bytes 294912 | tf_op jit(solution)/shard_map/all_to_all | solution.py:180
  52.4 20.4 %copy-start.11 = (f32[32,2,4,160]{3,2,1,0:T(4,128)S(1)}, f32[32,2,4,160]{3,2,1,0:T(4,128)}, u32[]{:S(2)}) copy-start(f32[32,2,4,160]{3,2,1,0:T(4,128)} %get-tuple-element.25) | copy-start | bytes 491524
  54.0 16.6 %all-to-all-start.1 = ((f32[32,2,1152]{2,1,0:T(2,128)}), f32[32,2,1152]{2,1,0:T(2,128)S(1)}, u32[]{:S(2)}, u32[]{:S(2)}) async-start(f32[32,2,1152]{2,1,0:T(2,128)} %concatenate.26), calls=%async_computation.1 | async-start | bytes 589824 | tf_op jit(solution)/shard_map/all_to_all | solution.py:206
  75.5 21.5 %copy-start.15 = (f32[5120]{0:T(1024)S(1)}, f32[5120]{0:T(1024)}, u32[]{:S(2)}) copy-start(f32[5120]{0:T(1024)} %param.28) | copy-start | bytes 61444
  82.1 13.1 %all-to-all-start.2 = ((bf16[4,8,5120]{2,1,0:T(8,128)(2,1)}), bf16[4,8,5120]{2,1,0:T(8,128)(2,1)S(1)}, u32[]{:S(2)}, u32[]{:S(2)}) async-start(bf16[4,8,5120]{2,1,0:T(8,128)(2,1)} %fusion), calls=%async_computation.2 | async-start | bytes 655360 | tf_op jit(solution)/shard_map/all_to_all | solution.py:271
  87.4 60.5 %collective-permute-start.6 = (bf16[5120,256]{1,0:T(8,128)(2,1)}, bf16[5120,256]{1,0:T(8,128)(2,1)}, u32[]{:S(2)}, u32[]{:S(2)}) collective-permute-start(bf16[5120,256]{1,0:T(8,128)(2,1)} %refs_2_.3), channel_id=1, source_target_pairs={{0,4},{4,0},{1,5},{5,1},{2,6},{6,2},{3,7},{7,3},{8,12},{12,8},{9,1... | collective-permute-start | bytes 7864328 | tf_op jit(solution)/shard_map/ppermute | solution.py:26
  87.4 61.5 %collective-permute-start.7 = (bf16[5120,256]{1,0:T(8,128)(2,1)}, bf16[5120,256]{1,0:T(8,128)(2,1)}, u32[]{:S(2)}, u32[]{:S(2)}) collective-permute-start(bf16[5120,256]{1,0:T(8,128)(2,1)} %refs_4_.5), channel_id=1, source_target_pairs={{0,4},{4,0},{1,5},{5,1},{2,6},{6,2},{3,7},{7,3},{8,12},{12,8},{9,1... | collective-permute-start | bytes 7864328 | tf_op jit(solution)/shard_map/ppermute | solution.py:26
  87.9 118.0 %collective-permute-start.23 = (bf16[1024,1280]{1,0:T(8,128)(2,1)}, bf16[1024,1280]{1,0:T(8,128)(2,1)}, u32[]{:S(2)}, u32[]{:S(2)}) collective-permute-start(bf16[1024,1280]{1,0:T(8,128)(2,1)} %refs_12_.1), channel_id=1, source_target_pairs={{0,4},{4,0},{1,5},{5,1},{2,6},{6,2},{3,7},{7,3},{8,12},{12,8},{9,1... | collective-permute-start | bytes 7864328 | tf_op jit(solution)/shard_map/ppermute | solution.py:26
  109.7 5.4 %collective-permute-start.2 = (bf16[16,5120]{1,0:T(8,128)(2,1)S(1)}, bf16[16,5120]{1,0:T(8,128)(2,1)S(1)}, u32[]{:S(2)}, u32[]{:S(2)}) collective-permute-start(bf16[16,5120]{1,0:T(8,128)(2,1)S(1)} %get-tuple-element.17), channel_id=1, source_target_pairs={{0,24},{8,0},{16,8},{24,16},{1,25},{9,1},{17,9},{25,17},{2,26},{10... | collective-permute-start | bytes 491528 | tf_op jit(solution)/shard_map/ppermute | solution.py:26
  111.2 8.0 %collective-permute-start.1 = (bf16[16,5120]{1,0:T(8,128)(2,1)S(1)}, bf16[16,5120]{1,0:T(8,128)(2,1)S(1)}, u32[]{:S(2)}, u32[]{:S(2)}) collective-permute-start(bf16[16,5120]{1,0:T(8,128)(2,1)S(1)} %get-tuple-element.17), channel_id=1, source_target_pairs={{0,16},{8,24},{16,0},{24,8},{1,17},{9,25},{17,1},{25,9},{2,18},{10... | collective-permute-start | bytes 491528 | tf_op jit(solution)/shard_map/ppermute | solution.py:26
  115.0 6.5 %collective-permute-start = (bf16[16,5120]{1,0:T(8,128)(2,1)S(1)}, bf16[16,5120]{1,0:T(8,128)(2,1)S(1)}, u32[]{:S(2)}, u32[]{:S(2)}) collective-permute-start(bf16[16,5120]{1,0:T(8,128)(2,1)S(1)} %get-tuple-element.17), channel_id=1, source_target_pairs={{0,8},{8,16},{16,24},{24,0},{1,9},{9,17},{17,25},{25,1},{2,10},{10... | collective-permute-start | bytes 491528 | tf_op jit(solution)/shard_map/ppermute | solution.py:26
  119.1 6.2 %collective-permute-start.5 = (bf16[16,5120]{1,0:T(8,128)(2,1)S(1)}, bf16[16,5120]{1,0:T(8,128)(2,1)S(1)}, u32[]{:S(2)}, u32[]{:S(2)}) collective-permute-start(bf16[16,5120]{1,0:T(8,128)(2,1)S(1)} %get-tuple-element.16), channel_id=1, source_target_pairs={{0,96},{32,0},{64,32},{96,64},{1,97},{33,1},{65,33},{97,65},{2,98}... | collective-permute-start | bytes 491528 | tf_op jit(solution)/shard_map/ppermute | solution.py:26
  121.6 7.1 %collective-permute-start.4 = (bf16[16,5120]{1,0:T(8,128)(2,1)S(1)}, bf16[16,5120]{1,0:T(8,128)(2,1)S(1)}, u32[]{:S(2)}, u32[]{:S(2)}) collective-permute-start(bf16[16,5120]{1,0:T(8,128)(2,1)S(1)} %get-tuple-element.16), channel_id=1, source_target_pairs={{0,64},{32,96},{64,0},{96,32},{1,65},{33,97},{65,1},{97,33},{2,66}... | collective-permute-start | bytes 491528 | tf_op jit(solution)/shard_map/ppermute | solution.py:26
  125.3 8.3 %collective-permute-start.3 = (bf16[16,5120]{1,0:T(8,128)(2,1)S(1)}, bf16[16,5120]{1,0:T(8,128)(2,1)S(1)}, u32[]{:S(2)}, u32[]{:S(2)}) collective-permute-start(bf16[16,5120]{1,0:T(8,128)(2,1)S(1)} %get-tuple-element.16), channel_id=1, source_target_pairs={{0,32},{32,64},{64,96},{96,0},{1,33},{33,65},{65,97},{97,1},{2,34}... | collective-permute-start | bytes 491528 | tf_op jit(solution)/shard_map/ppermute | solution.py:26
  126.9 22.1 %copy-start.2 = (bf16[64,5120]{1,0:T(8,128)(2,1)}, bf16[64,5120]{1,0:T(8,128)(2,1)S(1)}, u32[]{:S(2)}) copy-start(bf16[64,5120]{1,0:T(8,128)(2,1)S(1)} %pad_maximum_fusion.refs_0_) | copy-start | bytes 1966084
  128.7 16.0 %collective-permute-start.11 = (bf16[64,5120]{1,0:T(8,128)(2,1)S(1)}, bf16[64,5120]{1,0:T(8,128)(2,1)S(1)}, u32[]{:S(2)}, u32[]{:S(2)}) collective-permute-start(bf16[64,5120]{1,0:T(8,128)(2,1)S(1)} %pad_maximum_fusion.refs_0_), channel_id=1, source_target_pairs={{0,32},{32,64},{64,96},{96,0},{1,33},{33,65},{65,97},{97,1},{2,34}... | collective-permute-start | bytes 1966088 | tf_op jit(solution)/shard_map/ppermute | solution.py:26
  133.7 11.0 %collective-permute-start.12 = (bf16[64,5120]{1,0:T(8,128)(2,1)S(1)}, bf16[64,5120]{1,0:T(8,128)(2,1)S(1)}, u32[]{:S(2)}, u32[]{:S(2)}) collective-permute-start(bf16[64,5120]{1,0:T(8,128)(2,1)S(1)} %pad_maximum_fusion.refs_0_), channel_id=1, source_target_pairs={{0,96},{32,0},{64,32},{96,64},{1,97},{33,1},{65,33},{97,65},{2,98}... | collective-permute-start | bytes 1966088 | tf_op jit(solution)/shard_map/ppermute | solution.py:26
  144.6 29.2 %collective-permute-start.13 = (bf16[64,5120]{1,0:T(8,128)(2,1)}, bf16[64,5120]{1,0:T(8,128)(2,1)}, u32[]{:S(2)}, u32[]{:S(2)}) collective-permute-start(bf16[64,5120]{1,0:T(8,128)(2,1)} %pad_maximum_fusion.1.refs_1_), channel_id=1, source_target_pairs={{0,8},{8,16},{16,24},{24,0},{1,9},{9,17},{17,25},{25,1},{2,10},{10... | collective-permute-start | bytes 1966088 | tf_op jit(solution)/shard_map/ppermute | solution.py:26
  144.7 29.2 %collective-permute-start.14 = (bf16[64,5120]{1,0:T(8,128)(2,1)}, bf16[64,5120]{1,0:T(8,128)(2,1)}, u32[]{:S(2)}, u32[]{:S(2)}) collective-permute-start(bf16[64,5120]{1,0:T(8,128)(2,1)} %pad_maximum_fusion.1.refs_1_), channel_id=1, source_target_pairs={{0,24},{8,0},{16,8},{24,16},{1,25},{9,1},{17,9},{25,17},{2,26},{10... | collective-permute-start | bytes 1966088 | tf_op jit(solution)/shard_map/ppermute | solution.py:26
  147.9 43.3 %collective-permute-start.18 = (bf16[64,5120]{1,0:T(8,128)(2,1)S(1)}, bf16[64,5120]{1,0:T(8,128)(2,1)}, u32[]{:S(2)}, u32[]{:S(2)}) collective-permute-start(bf16[64,5120]{1,0:T(8,128)(2,1)S(1)} %pad_maximum_fusion.refs_0_), channel_id=1, source_target_pairs={{0,64},{32,96},{64,0},{96,32},{1,65},{33,97},{65,1},{97,33},{2,66}... | collective-permute-start | bytes 1966088 | tf_op jit(solution)/shard_map/ppermute | solution.py:26
  148.9 44.2 %collective-permute-start.19 = (bf16[64,5120]{1,0:T(8,128)(2,1)}, bf16[64,5120]{1,0:T(8,128)(2,1)}, u32[]{:S(2)}, u32[]{:S(2)}) collective-permute-start(bf16[64,5120]{1,0:T(8,128)(2,1)} %pad_maximum_fusion.1.refs_1_), channel_id=1, source_target_pairs={{0,16},{8,24},{16,0},{24,8},{1,17},{9,25},{17,1},{25,9},{2,18},{10... | collective-permute-start | bytes 1966088 | tf_op jit(solution)/shard_map/ppermute | solution.py:26
  173.9 34.1 %collective-permute-start.8 = (bf16[128,512]{1,0:T(8,128)(2,1)}, bf16[128,512]{1,0:T(8,128)(2,1)}, u32[]{:S(2)}, u32[]{:S(2)}) collective-permute-start(bf16[128,512]{1,0:T(8,128)(2,1)} %mlp_in.3.refs_0_), channel_id=1, source_target_pairs={{0,1},{1,2},{2,3},{3,0},{4,5},{5,6},{6,7},{7,4},{8,9},{9,10},{10,1... | collective-permute-start | bytes 393224 | tf_op jit(solution)/shard_map/ppermute | solution.py:26
  173.9 36.8 %collective-permute-start.9 = (bf16[128,512]{1,0:T(8,128)(2,1)}, bf16[128,512]{1,0:T(8,128)(2,1)}, u32[]{:S(2)}, u32[]{:S(2)}) collective-permute-start(bf16[128,512]{1,0:T(8,128)(2,1)} %mlp_in.3.refs_0_), channel_id=1, source_target_pairs={{0,2},{1,3},{2,0},{3,1},{4,6},{5,7},{6,4},{7,5},{8,10},{9,11},{10,... | collective-permute-start | bytes 393224 | tf_op jit(solution)/shard_map/ppermute | solution.py:26
  191.2 19.5 %collective-permute-start.10 = (bf16[128,512]{1,0:T(8,128)(2,1)}, bf16[128,512]{1,0:T(8,128)(2,1)S(1)}, u32[]{:S(2)}, u32[]{:S(2)}) collective-permute-start(bf16[128,512]{1,0:T(8,128)(2,1)} %mlp_in.3.refs_0_), channel_id=1, source_target_pairs={{0,3},{1,0},{2,1},{3,2},{4,7},{5,4},{6,5},{7,6},{8,11},{9,8},{10,9... | collective-permute-start | bytes 393224 | tf_op jit(solution)/shard_map/ppermute | solution.py:26
  193.2 30.6 %collective-permute-start.15 = (bf16[256,512]{1,0:T(8,128)(2,1)}, bf16[256,512]{1,0:T(8,128)(2,1)S(1)}, u32[]{:S(2)}, u32[]{:S(2)}) collective-permute-start(bf16[256,512]{1,0:T(8,128)(2,1)} %mlp_in.4.refs_4_), channel_id=1, source_target_pairs={{0,1},{1,2},{2,3},{3,0},{4,5},{5,6},{6,7},{7,4},{8,9},{9,10},{10,1... | collective-permute-start | bytes 786440 | tf_op jit(solution)/shard_map/ppermute | solution.py:26
  206.0 17.8 %collective-permute-start.16 = (bf16[256,512]{1,0:T(8,128)(2,1)S(1)}, bf16[256,512]{1,0:T(8,128)(2,1)S(1)}, u32[]{:S(2)}, u32[]{:S(2)}) collective-permute-start(bf16[256,512]{1,0:T(8,128)(2,1)S(1)} %copy-done.3), channel_id=1, source_target_pairs={{0,2},{1,3},{2,0},{3,1},{4,6},{5,7},{6,4},{7,5},{8,10},{9,11},{10,... | collective-permute-start | bytes 786440 | tf_op jit(solution)/shard_map/ppermute | solution.py:26
  208.0 15.8 %collective-permute-start.17 = (bf16[256,512]{1,0:T(8,128)(2,1)S(1)}, bf16[256,512]{1,0:T(8,128)(2,1)}, u32[]{:S(2)}, u32[]{:S(2)}) collective-permute-start(bf16[256,512]{1,0:T(8,128)(2,1)S(1)} %copy-done.3), channel_id=1, source_target_pairs={{0,3},{1,0},{2,1},{3,2},{4,7},{5,4},{6,5},{7,6},{8,11},{9,8},{10,9... | collective-permute-start | bytes 786440 | tf_op jit(solution)/shard_map/ppermute | solution.py:26
  210.6 7.9 %collective-permute-start.20 = (bf16[128,512]{1,0:T(8,128)(2,1)}, bf16[128,512]{1,0:T(8,128)(2,1)}, u32[]{:S(2)}, u32[]{:S(2)}) collective-permute-start(bf16[128,512]{1,0:T(8,128)(2,1)} %mlp_in.5.refs_8_), channel_id=1, source_target_pairs={{0,1},{1,2},{2,3},{3,0},{4,5},{5,6},{6,7},{7,4},{8,9},{9,10},{10,1... | collective-permute-start | bytes 393224 | tf_op jit(solution)/shard_map/ppermute | solution.py:26
  210.7 8.6 %collective-permute-start.21 = (bf16[128,512]{1,0:T(8,128)(2,1)}, bf16[128,512]{1,0:T(8,128)(2,1)}, u32[]{:S(2)}, u32[]{:S(2)}) collective-permute-start(bf16[128,512]{1,0:T(8,128)(2,1)} %mlp_in.5.refs_8_), channel_id=1, source_target_pairs={{0,2},{1,3},{2,0},{3,1},{4,6},{5,7},{6,4},{7,5},{8,10},{9,11},{10,... | collective-permute-start | bytes 393224 | tf_op jit(solution)/shard_map/ppermute | solution.py:26
  218.5 5.3 %collective-permute-start.22 = (bf16[128,512]{1,0:T(8,128)(2,1)}, bf16[128,512]{1,0:T(8,128)(2,1)}, u32[]{:S(2)}, u32[]{:S(2)}) collective-permute-start(bf16[128,512]{1,0:T(8,128)(2,1)} %mlp_in.5.refs_8_), channel_id=1, source_target_pairs={{0,3},{1,0},{2,1},{3,2},{4,7},{5,4},{6,5},{7,6},{8,11},{9,8},{10,9... | collective-permute-start | bytes 393224 | tf_op jit(solution)/shard_map/ppermute | solution.py:26
  232.4 21.2 %copy-start.6 = (bf16[8,5120]{1,0:T(8,128)(2,1)S(1)}, bf16[8,5120]{1,0:T(8,128)(2,1)}, u32[]{:S(2)}) copy-start(bf16[8,5120]{1,0:T(8,128)(2,1)} %copy-done.5) | copy-start | bytes 245764
  (13 other events, 119.5 us)

commit v3 on v2

--- a/solution.py
+++ b/solution.py
@@ -285,7 +285,10 @@
         * lax.rsqrt(jnp.mean(resid_f * resid_f, axis=-1, keepdims=True) + 1e-05)
         * norm_gain
     ).astype(jnp.bfloat16)
-    block = lax.all_gather(normed, "head", axis=0, tiled=True)
+    from_head = ring_pieces(normed, "head")
+    block = jnp.concatenate(
+        [lax.select_n((head_index - i) % n_head, *from_head) for i in range(RING)], axis=0
+    )
     half = row_count // 2
     first_a = jnp.concatenate(ring_pieces(block[:half], "x"), axis=0)
     first_b = jnp.concatenate(ring_pieces(block[half:], "y"), axis=0)

time: 256 us -> 252 us (0.984)
  blocking collectives: 33.6 us -> 23.3 us
  starting transfers between devices: 45 us -> 49.3 us
  local copies, waits for them, and re-layouts: 26.6 us -> 29.9 us
    all_gather x1 -> x0, blocking collectives: 12.6 us -> none  [shards(): block = lax.all_gather(normed, 'head', axis=0, tiled=True)]
    ppermute x24 -> x27, starting transfers between devices: 25 us -> 29.2 us  [shift(): lax.ppermute(value, axis, [(i, (i + step) % size) for i in range(size)])]
    ppermute x24 -> x27, waiting for transfers between devices: 47.4 us -> 44.8 us  [shift(): lax.ppermute(value, axis, [(i, (i + step) % size) for i in range(size)])]
  transfers between devices with their start and end apart: 27 -> 30, of which waited for: 12 -> 15; matrix products, arithmetic and copies ran while one was open for 13% -> 14% of each run, Pallas kernels for 16% -> 16%
where the time goes in v3:
time: 252 us; the launch traced here: 250 us
  waiting for transfers between devices  61.1 us (24%)
  starting transfers between devices  49.3 us (20%)
  Pallas kernels  48.2 us (19%)
  local copies, waits for them, and re-layouts  29.9 us (12%)
  blocking collectives  23.3 us (9%)
  matrix products  19.8 us (8%)
  other arithmetic  18 us (7%)
    ppermute x27, waiting for transfers between devices, shift(): lax.ppermute(value, axis, [(i, (i + step) % size) for i in range(size)])  44.8 us
    pallas_call x3, Pallas kernels, mlp_in(): pl.pallas_call(functools.partial(mlp_in_kernel, n=n), grid=(depth // K_BL...  40.5 us
    ppermute x27, starting transfers between devices, shift(): lax.ppermute(value, axis, [(i, (i + step) % size) for i in range(size)])  29.2 us
    all_to_all x1, blocking collectives, shards(): lax.all_to_all(partial.reshape(RING * RING * n_head, sub_rows, -1), ('y',...  23.3 us
    all_to_all x1, waiting for transfers between devices, shards(): lax.all_to_all(jnp.concatenate([mixture.reshape(slot_total, col_width), l...  8.57 us
    all_to_all x1, waiting for transfers between devices, shards(): lax.all_to_all(projected.astype(jnp.bfloat16).reshape(n_head, sub_rows, -...  7.77 us
    pallas_call x1, Pallas kernels, mlp_out(): pl.pallas_call(functools.partial(mlp_out_kernel, groups=groups), grid_spe...  7.76 us
    all_to_all x1, starting transfers between devices, shards(): lax.all_to_all(sent_rows.reshape(n_req, slot_cap, col_width + HEAD_WIDTH)...  7.4 us
  transfers between devices with their start and end apart: 30, of which 15 were waited for; matrix products, arithmetic and copies ran while one was open for 14% of the time, Pallas kernels for 16%

profile of v3, /device:TPU:0, one launch (start us, length us, event | category | flops | bytes accessed | tf_op | source)
XLA Modules:
  0.0 250.1 jit_solution(4079607231249342610)
XLA Ops:
  4.1 7.4 %all-to-all-start = ((bf16[32,2,1152]{2,1,0:T(2,128)(2,1)}), bf16[32,2,1152]{2,1,0:T(2,128)(2,1)S(1)}, u32[]{:S(2)}, u32[]{:S(2)}) async-start(bf16[32,2,1152]{2,1,0:T(2,128)(2,1)} %reshape.252), calls=%async_computation | async-start | bytes 294912 | tf_op jit(solution)/shard_map/all_to_all | solution.py:180
  18.8 3.6 %fusion.76 = (f32[32,2,4]{2,1,0:T(2,128)}, f32[32,2,4,160]{3,2,1,0:T(4,128)}) fusion(bf16[32,2,4,128]{3,2,1,0:T(4,128)(2,1)} %reshape.261, pred[32,160]{1,0:T(8,128)(4,1)} %iota_compare_fusion, bf16[32,160,256]{2,1,0:T(8,128)(2,1)S(1)} %copy-done), kind=kOutput, calls=%fused_computation.118 | convolution fusion | flops 10608384 | bytes 2856960 | tf_op jit(solution)/shard_map/bkrd,btkd->bkrt/dot_general | solution.py:233
  33.3 2.0 reshape.257
  45.0 3.5 %fusion.75 = (f32[64,2,4]{0,2,1:T(4,128)S(1)}, f32[64,2,4,1536]{3,0,2,1:T(8,128)}) fusion(bf16[1536,2,128,1]{2,1,0,3:T(2,128)(2,1)} %bitcast.65, bf16[64,2,4,128]{3,2,1,0:T(4,128)(2,1)S(1)} %reshape.255, pred[64,1536]{1,0:T(8,128)(4,1)S(1)} %compare_and_fusion), kind=kOutput, calls=%fused_computation.117 | convolution fusion | flops 203685376 | bytes 4163584 | tf_op jit(solution)/shard_map/nkrd,pkd->nkrp/dot_general | solution.py:190
  48.6 2.6 %fusion.3 = f32[64,2,4]{0,2,1:T(4,128)S(1)} fusion(f32[64,2,4,1536]{3,0,2,1:T(8,128)} %get-tuple-element.33, f32[64,2,4]{0,2,1:T(4,128)S(1)} %get-tuple-element.32), kind=kLoop, calls=%fused_computation.7 | loop fusion | flops 1572352 | bytes 3149824 | tf_op jit(solution)/shard_map/reduce_sum | solution.py:199
  54.0 7.4 %all-to-all-start.1 = ((f32[32,2,1152]{2,1,0:T(2,128)}), f32[32,2,1152]{2,1,0:T(2,128)S(1)}, u32[]{:S(2)}, u32[]{:S(2)}) async-start(f32[32,2,1152]{2,1,0:T(2,128)} %concatenate.35), calls=%async_computation.1 | async-start | bytes 589824 | tf_op jit(solution)/shard_map/all_to_all | solution.py:206
  62.0 8.6 %all-to-all-done.1 = f32[32,2,1152]{2,1,0:T(2,128)S(1)} async-done(((f32[32,2,1152]{2,1,0:T(2,128)}), f32[32,2,1152]{2,1,0:T(2,128)S(1)}, u32[]{:S(2)}, u32[]{:S(2)}) %all-to-all-start.1) | async-done | bytes 294944 | tf_op jit(solution)/shard_map/all_to_all | solution.py:206
  72.8 2.6 %fusion.35 = bf16[32,2,4,128]{3,2,1,0:T(4,128)(2,1)S(1)} fusion(f32[32,2,4,160]{3,2,1,0:T(4,128)S(1)} %copy-done.7, f32[32,2,4]{2,1,0:T(2,128)} %copy.74, f32[32,2,4,128]{3,2,1,0:T(4,128)S(1)} %reshape.259, f32[32,2,4]{2,1,0:T(2,128)S(1)} %copy.80, f32[32,2,4]{2,1,0:T(2,128)S(1)} %copy.77, f32[32,2,128]{2,1,0:T(2,128)} %reshape.269, f32[32,2,4]{2,1,0:T(2,128)} %copy.76, ...), kind=kOutput, calls=%fused_computation.26 | convolution fusion | flops 10797056 | bytes 3019776 | tf_op jit(solution)/shard_map/bkrt,btkd->bkrd/dot_general | solution.py:254
  75.5 6.6 %fusion = bf16[4,8,5120]{2,1,0:T(8,128)(2,1)} fusion(bf16[32,1024]{1,0:T(8,128)(2,1)S(1)} %convert_element_type.82, bf16[1024,5120]{1,0:T(8,128)(2,1)} %param.27), kind=kOutput, calls=%fused_computation.2 | convolution fusion | flops 335708160 | bytes 10878976 | tf_op jit(solution)/shard_map/dot_general | solution.py:268
  82.1 5.3 %all-to-all-start.2 = ((bf16[4,8,5120]{2,1,0:T(8,128)(2,1)}), bf16[4,8,5120]{2,1,0:T(8,128)(2,1)S(1)}, u32[]{:S(2)}, u32[]{:S(2)}) async-start(bf16[4,8,5120]{2,1,0:T(8,128)(2,1)} %fusion), calls=%async_computation.2 | async-start | bytes 655360 | tf_op jit(solution)/shard_map/all_to_all | solution.py:271
  87.4 7.8 %all-to-all-done.2 = bf16[4,8,5120]{2,1,0:T(8,128)(2,1)S(1)} async-done(((bf16[4,8,5120]{2,1,0:T(8,128)(2,1)}), bf16[4,8,5120]{2,1,0:T(8,128)(2,1)S(1)}, u32[]{:S(2)}, u32[]{:S(2)}) %all-to-all-start.2) | async-done | bytes 327712 | tf_op jit(solution)/shard_map/all_to_all | solution.py:271
  97.0 2.7 %collective-permute-start.2 = (bf16[8,5120]{1,0:T(8,128)(2,1)S(1)}, bf16[8,5120]{1,0:T(8,128)(2,1)S(1)}, u32[]{:S(2)}, u32[]{:S(2)}) collective-permute-start(bf16[8,5120]{1,0:T(8,128)(2,1)S(1)} %fusion.44), channel_id=1, source_target_pairs={{0,3},{1,0},{2,1},{3,2},{4,7},{5,4},{6,5},{7,6},{8,11},{9,8},{10,9... | collective-permute-start | bytes 245768 | tf_op jit(solution)/shard_map/ppermute | solution.py:26
  100.2 2.5 collective-permute-done.1
  102.7 2.7 %collective-permute-done = bf16[8,5120]{1,0:T(8,128)(2,1)S(1)} collective-permute-done((bf16[8,5120]{1,0:T(8,128)(2,1)S(1)}, bf16[8,5120]{1,0:T(8,128)(2,1)S(1)}, u32[]{:S(2)}, u32[]{:S(2)}) %collective-permute-start) | collective-permute-done | bytes 81952 | tf_op jit(solution)/shard_map/ppermute | solution.py:26
  107.8 2.1 collective-permute-start.4
  110.0 6.0 %collective-permute-done.3 = bf16[16,5120]{1,0:T(8,128)(2,1)S(1)} collective-permute-done((bf16[16,5120]{1,0:T(8,128)(2,1)S(1)}, bf16[16,5120]{1,0:T(8,128)(2,1)S(1)}, u32[]{:S(2)}, u32[]{:S(2)}) %collective-permute-start.3) | collective-permute-done | bytes 163872 | tf_op jit(solution)/shard_map/ppermute | solution.py:26
  118.3 2.9 %collective-permute-done.5 = bf16[16,5120]{1,0:T(8,128)(2,1)S(1)} collective-permute-done((bf16[16,5120]{1,0:T(8,128)(2,1)S(1)}, bf16[16,5120]{1,0:T(8,128)(2,1)S(1)}, u32[]{:S(2)}, u32[]{:S(2)}) %collective-permute-start.5) | collective-permute-done | bytes 163872 | tf_op jit(solution)/shard_map/ppermute | solution.py:26
  126.3 2.8 %collective-permute-done.7 = bf16[16,5120]{1,0:T(8,128)(2,1)S(1)} collective-permute-done((bf16[16,5120]{1,0:T(8,128)(2,1)S(1)}, bf16[16,5120]{1,0:T(8,128)(2,1)S(1)}, u32[]{:S(2)}, u32[]{:S(2)}) %collective-permute-start.7) | collective-permute-done | bytes 163872 | tf_op jit(solution)/shard_map/ppermute | solution.py:26
  130.9 3.0 %collective-permute-start.15 = (bf16[64,5120]{1,0:T(8,128)(2,1)}, bf16[64,5120]{1,0:T(8,128)(2,1)}, u32[]{:S(2)}, u32[]{:S(2)}) collective-permute-start(bf16[64,5120]{1,0:T(8,128)(2,1)} %constant_dynamic-update-slice_fusion.refs_0_), channel_id=1, source_target_pairs={{0,96},{32,0},{64,32},{96,64},{1,97},{33,1},{65,33},{97,65},{2,98}... | collective-permute-start | bytes 1966088 | tf_op jit(solution)/shard_map/ppermute | solution.py:26
  135.2 7.0 %collective-permute-done.14.refs_0_ = bf16[64,5120]{1,0:T(8,128)(2,1)S(1)} collective-permute-done((bf16[64,5120]{1,0:T(8,128)(2,1)}, bf16[64,5120]{1,0:T(8,128)(2,1)S(1)}, u32[]{:S(2)}, u32[]{:S(2)}) %collective-permute-start.14) | collective-permute-done | bytes 655392 | tf_op jit(solution)/shard_map/ppermute | solution.py:26
  142.2 7.6 %collective-permute-done.15.refs_1_ = bf16[64,5120]{1,0:T(8,128)(2,1)} collective-permute-done((bf16[64,5120]{1,0:T(8,128)(2,1)}, bf16[64,5120]{1,0:T(8,128)(2,1)}, u32[]{:S(2)}, u32[]{:S(2)}) %collective-permute-start.15) | collective-permute-done | bytes 655392 | tf_op jit(solution)/shard_map/ppermute | solution.py:26
  151.7 12.7 %mlp_in.3.refs_0_ = bf16[128,512]{1,0:T(8,128)(2,1)} custom-call(bf16[64,5120]{1,0:T(8,128)(2,1)} %constant_dynamic-update-slice_fusion.refs_0_, bf16[64,5120]{1,0:T(8,128)(2,1)} %constant_dynamic-update-slice_fusion.5.refs_1_, bf16[5120,256]{1,0:T(8,128)(2,1)} %refs_2_.3, bf16[5120,256]{1,0:T(8,128)(2,1)} %collective-permute-done.9.refs_3_.refs_5_, ...), custom_call_target="tpu_custom_call" | custom-call | tf_op jit(solution)/shard_map/mlp_in/pallas_call | solution.py:60
  164.4 4.0 %collective-permute-done.16.refs_2_ = bf16[64,5120]{1,0:T(8,128)(2,1)} collective-permute-done((bf16[64,5120]{1,0:T(8,128)(2,1)}, bf16[64,5120]{1,0:T(8,128)(2,1)}, u32[]{:S(2)}, u32[]{:S(2)}) %collective-permute-start.16) | collective-permute-done | bytes 655392 | tf_op jit(solution)/shard_map/ppermute | solution.py:26
  168.4 2.9 %collective-permute-start.11 = (bf16[128,512]{1,0:T(8,128)(2,1)}, bf16[128,512]{1,0:T(8,128)(2,1)S(1)}, u32[]{:S(2)}, u32[]{:S(2)}) collective-permute-start(bf16[128,512]{1,0:T(8,128)(2,1)} %mlp_in.3.refs_0_), channel_id=1, source_target_pairs={{0,1},{1,2},{2,3},{3,0},{4,5},{5,6},{6,7},{7,4},{8,9},{9,10},{10,1... | collective-permute-start | bytes 393224 | tf_op jit(solution)/shard_map/ppermute | solution.py:26
  171.4 15.1 %mlp_in.4.refs_4_ = bf16[256,512]{1,0:T(8,128)(2,1)} custom-call(bf16[64,5120]{1,0:T(8,128)(2,1)} %copy-done.4, bf16[64,5120]{1,0:T(8,128)(2,1)} %collective-permute-done.15.refs_1_, bf16[64,5120]{1,0:T(8,128)(2,1)} %collective-permute-done.16.refs_2_, bf16[64,5120]{1,0:T(8,128)(2,1)} %collective-permute-done.17.refs_3_, bf16[5120,256]{1,0:T(8,128)(2,1)} %refs_2_.3, ...), custom_call_target="tpu_custom_call" | custom-call | tf_op jit(solution)/shard_map/mlp_in/pallas_call | solution.py:60
  186.5 2.7 %collective-permute-start.13 = (bf16[128,512]{1,0:T(8,128)(2,1)S(1)}, bf16[128,512]{1,0:T(8,128)(2,1)}, u32[]{:S(2)}, u32[]{:S(2)}) collective-permute-start(bf16[128,512]{1,0:T(8,128)(2,1)S(1)} %copy-done.5), channel_id=1, source_target_pairs={{0,3},{1,0},{2,1},{3,2},{4,7},{5,4},{6,5},{7,6},{8,11},{9,8},{10,9... | collective-permute-start | bytes 393224 | tf_op jit(solution)/shard_map/ppermute | solution.py:26
  189.3 12.7 %mlp_in.5.refs_8_ = bf16[128,512]{1,0:T(8,128)(2,1)} custom-call(bf16[64,5120]{1,0:T(8,128)(2,1)} %collective-permute-done.21.refs_0_, bf16[64,5120]{1,0:T(8,128)(2,1)} %collective-permute-done.22.refs_1_, bf16[5120,256]{1,0:T(8,128)(2,1)} %refs_2_.3, bf16[5120,256]{1,0:T(8,128)(2,1)} %collective-permute-done.9.refs_3_.refs_5_, bf16[5120,256]{1,0:T(8,128)(2,1)} %refs_4_.5, ...), custom_call_target="tpu_custom_call" | custom-call | tf_op jit(solution)/shard_map/mlp_in/pallas_call | solution.py:60
  202.0 2.9 %collective-permute-start.19 = (bf16[256,512]{1,0:T(8,128)(2,1)S(1)}, bf16[256,512]{1,0:T(8,128)(2,1)}, u32[]{:S(2)}, u32[]{:S(2)}) collective-permute-start(bf16[256,512]{1,0:T(8,128)(2,1)S(1)} %copy-done.2), channel_id=1, source_target_pairs={{0,2},{1,3},{2,0},{3,1},{4,6},{5,7},{6,4},{7,5},{8,10},{9,11},{10,... | collective-permute-start | bytes 786440 | tf_op jit(solution)/shard_map/ppermute | solution.py:26
  208.3 3.8 %collective-permute-done.23.refs_9_ = bf16[128,512]{1,0:T(8,128)(2,1)} collective-permute-done((bf16[128,512]{1,0:T(8,128)(2,1)}, bf16[128,512]{1,0:T(8,128)(2,1)}, u32[]{:S(2)}, u32[]{:S(2)}) %collective-permute-start.23) | collective-permute-done | bytes 131104 | tf_op jit(solution)/shard_map/ppermute | solution.py:26
  213.7 3.7 %collective-permute-done.25.refs_11_ = bf16[128,512]{1,0:T(8,128)(2,1)} collective-permute-done((bf16[128,512]{1,0:T(8,128)(2,1)}, bf16[128,512]{1,0:T(8,128)(2,1)}, u32[]{:S(2)}, u32[]{:S(2)}) %collective-permute-start.25) | collective-permute-done | bytes 131104 | tf_op jit(solution)/shard_map/ppermute | solution.py:26
  218.1 7.8 %mlp_out.1 = bf16[16,32,1280]{2,1,0:T(8,128)(2,1)} custom-call(s32[36]{0:T(128)} %pad_add_fusion.index, bf16[128,512]{1,0:T(8,128)(2,1)} %mlp_in.3.refs_0_, bf16[128,512]{1,0:T(8,128)(2,1)} %copy-done.9, bf16[128,512]{1,0:T(8,128)(2,1)} %collective-permute-done.12.refs_2_, bf16[128,512]{1,0:T(8,128)(2,1)} %collective-permute-done.13.refs_3_, ...), custom_call_target="tpu_custom_call" | custom-call | tf_op jit(solution)/shard_map/mlp_out/pallas_call | solution.py:104
  225.9 23.3 %all_to_all.20 = bf16[64,8,1280]{2,1,0:T(8,128)(2,1)S(1)} all-to-all(bf16[64,8,1280]{2,1,0:T(8,128)(2,1)} %bitcast.62), channel_id=1, replica_groups=mesh['y'=4,'x'=4,'core'=2,'head'=4] {'y','x','head'}, dimensions={0} | all-to-all | bytes 2621440 | tf_op jit(solution)/shard_map/all_to_all | solution.py:314
  (145 shorter events, 61.5 us)
Async XLA Ops:
  0.0 32.2 %copy-start.3 = (bf16[3,512,256]{2,1,0:T(8,128)(2,1)S(1)}, bf16[3,512,256]{2,1,0:T(8,128)(2,1)}, u32[]{:S(2)}) copy-start(bf16[3,512,256]{2,1,0:T(8,128)(2,1)} %param.22) | copy-start | bytes 2359300
  4.1 35.9 %all-to-all-start = ((bf16[32,2,1152]{2,1,0:T(2,128)(2,1)}), bf16[32,2,1152]{2,1,0:T(2,128)(2,1)S(1)}, u32[]{:S(2)}, u32[]{:S(2)}) async-start(bf16[32,2,1152]{2,1,0:T(2,128)(2,1)} %reshape.252), calls=%async_computation | async-start | bytes 294912 | tf_op jit(solution)/shard_map/all_to_all | solution.py:180
  54.0 16.6 %all-to-all-start.1 = ((f32[32,2,1152]{2,1,0:T(2,128)}), f32[32,2,1152]{2,1,0:T(2,128)S(1)}, u32[]{:S(2)}, u32[]{:S(2)}) async-start(f32[32,2,1152]{2,1,0:T(2,128)} %concatenate.35), calls=%async_computation.1 | async-start | bytes 589824 | tf_op jit(solution)/shard_map/all_to_all | solution.py:206
  82.1 13.1 %all-to-all-start.2 = ((bf16[4,8,5120]{2,1,0:T(8,128)(2,1)}), bf16[4,8,5120]{2,1,0:T(8,128)(2,1)S(1)}, u32[]{:S(2)}, u32[]{:S(2)}) async-start(bf16[4,8,5120]{2,1,0:T(8,128)(2,1)} %fusion), calls=%async_computation.2 | async-start | bytes 655360 | tf_op jit(solution)/shard_map/all_to_all | solution.py:271
  96.4 6.3 %collective-permute-start.1 = (bf16[8,5120]{1,0:T(8,128)(2,1)S(1)}, bf16[8,5120]{1,0:T(8,128)(2,1)S(1)}, u32[]{:S(2)}, u32[]{:S(2)}) collective-permute-start(bf16[8,5120]{1,0:T(8,128)(2,1)S(1)} %fusion.44), channel_id=1, source_target_pairs={{0,2},{1,3},{2,0},{3,1},{4,6},{5,7},{6,4},{7,5},{8,10},{9,11},{10,... | collective-permute-start | bytes 245768 | tf_op jit(solution)/shard_map/ppermute | solution.py:26
  97.0 5.7 %collective-permute-start.2 = (bf16[8,5120]{1,0:T(8,128)(2,1)S(1)}, bf16[8,5120]{1,0:T(8,128)(2,1)S(1)}, u32[]{:S(2)}, u32[]{:S(2)}) collective-permute-start(bf16[8,5120]{1,0:T(8,128)(2,1)S(1)} %fusion.44), channel_id=1, source_target_pairs={{0,3},{1,0},{2,1},{3,2},{4,7},{5,4},{6,5},{7,6},{8,11},{9,8},{10,9... | collective-permute-start | bytes 245768 | tf_op jit(solution)/shard_map/ppermute | solution.py:26
  99.7 5.7 %collective-permute-start = (bf16[8,5120]{1,0:T(8,128)(2,1)S(1)}, bf16[8,5120]{1,0:T(8,128)(2,1)S(1)}, u32[]{:S(2)}, u32[]{:S(2)}) collective-permute-start(bf16[8,5120]{1,0:T(8,128)(2,1)S(1)} %fusion.44), channel_id=1, source_target_pairs={{0,1},{1,2},{2,3},{3,0},{4,5},{5,6},{6,7},{7,4},{8,9},{9,10},{10,1... | collective-permute-start | bytes 245768 | tf_op jit(solution)/shard_map/ppermute | solution.py:26
  99.7 51.2 %collective-permute-start.9 = (bf16[5120,256]{1,0:T(8,128)(2,1)}, bf16[5120,256]{1,0:T(8,128)(2,1)}, u32[]{:S(2)}, u32[]{:S(2)}) collective-permute-start(bf16[5120,256]{1,0:T(8,128)(2,1)} %refs_2_.3), channel_id=1, source_target_pairs={{0,4},{4,0},{1,5},{5,1},{2,6},{6,2},{3,7},{7,3},{8,12},{12,8},{9,1... | collective-permute-start | bytes 7864328 | tf_op jit(solution)/shard_map/ppermute | solution.py:26
  99.7 51.2 %collective-permute-start.10 = (bf16[5120,256]{1,0:T(8,128)(2,1)}, bf16[5120,256]{1,0:T(8,128)(2,1)}, u32[]{:S(2)}, u32[]{:S(2)}) collective-permute-start(bf16[5120,256]{1,0:T(8,128)(2,1)} %refs_4_.5), channel_id=1, source_target_pairs={{0,4},{4,0},{1,5},{5,1},{2,6},{6,2},{3,7},{7,3},{8,12},{12,8},{9,1... | collective-permute-start | bytes 7864328 | tf_op jit(solution)/shard_map/ppermute | solution.py:26
  102.7 99.3 %collective-permute-start.26 = (bf16[1024,1280]{1,0:T(8,128)(2,1)}, bf16[1024,1280]{1,0:T(8,128)(2,1)}, u32[]{:S(2)}, u32[]{:S(2)}) collective-permute-start(bf16[1024,1280]{1,0:T(8,128)(2,1)} %refs_12_.1), channel_id=1, source_target_pairs={{0,4},{4,0},{1,5},{5,1},{2,6},{6,2},{3,7},{7,3},{8,12},{12,8},{9,1... | collective-permute-start | bytes 7864328 | tf_op jit(solution)/shard_map/ppermute | solution.py:26
  107.0 9.0 %collective-permute-start.3 = (bf16[16,5120]{1,0:T(8,128)(2,1)S(1)}, bf16[16,5120]{1,0:T(8,128)(2,1)S(1)}, u32[]{:S(2)}, u32[]{:S(2)}) collective-permute-start(bf16[16,5120]{1,0:T(8,128)(2,1)S(1)} %pad_maximum_fusion), channel_id=1, source_target_pairs={{0,8},{8,16},{16,24},{24,0},{1,9},{9,17},{17,25},{25,1},{2,10},{10... | collective-permute-start | bytes 491528 | tf_op jit(solution)/shard_map/ppermute | solution.py:26
  107.8 8.8 %collective-permute-start.4 = (bf16[16,5120]{1,0:T(8,128)(2,1)S(1)}, bf16[16,5120]{1,0:T(8,128)(2,1)S(1)}, u32[]{:S(2)}, u32[]{:S(2)}) collective-permute-start(bf16[16,5120]{1,0:T(8,128)(2,1)S(1)} %pad_maximum_fusion), channel_id=1, source_target_pairs={{0,16},{8,24},{16,0},{24,8},{1,17},{9,25},{17,1},{25,9},{2,18},{10... | collective-permute-start | bytes 491528 | tf_op jit(solution)/shard_map/ppermute | solution.py:26
  116.0 5.3 %collective-permute-start.5 = (bf16[16,5120]{1,0:T(8,128)(2,1)S(1)}, bf16[16,5120]{1,0:T(8,128)(2,1)S(1)}, u32[]{:S(2)}, u32[]{:S(2)}) collective-permute-start(bf16[16,5120]{1,0:T(8,128)(2,1)S(1)} %pad_maximum_fusion), channel_id=1, source_target_pairs={{0,24},{8,0},{16,8},{24,16},{1,25},{9,1},{17,9},{25,17},{2,26},{10... | collective-permute-start | bytes 491528 | tf_op jit(solution)/shard_map/ppermute | solution.py:26
  116.6 7.2 %collective-permute-start.6 = (bf16[16,5120]{1,0:T(8,128)(2,1)S(1)}, bf16[16,5120]{1,0:T(8,128)(2,1)S(1)}, u32[]{:S(2)}, u32[]{:S(2)}) collective-permute-start(bf16[16,5120]{1,0:T(8,128)(2,1)S(1)} %pad_maximum_fusion.1), channel_id=1, source_target_pairs={{0,32},{32,64},{64,96},{96,0},{1,33},{33,65},{65,97},{97,1},{2,34}... | collective-permute-start | bytes 491528 | tf_op jit(solution)/shard_map/ppermute | solution.py:26
  121.3 7.8 %collective-permute-start.7 = (bf16[16,5120]{1,0:T(8,128)(2,1)S(1)}, bf16[16,5120]{1,0:T(8,128)(2,1)S(1)}, u32[]{:S(2)}, u32[]{:S(2)}) collective-permute-start(bf16[16,5120]{1,0:T(8,128)(2,1)S(1)} %pad_maximum_fusion.1), channel_id=1, source_target_pairs={{0,64},{32,96},{64,0},{96,32},{1,65},{33,97},{65,1},{97,33},{2,66}... | collective-permute-start | bytes 491528 | tf_op jit(solution)/shard_map/ppermute | solution.py:26
  123.8 7.1 %collective-permute-start.8 = (bf16[16,5120]{1,0:T(8,128)(2,1)S(1)}, bf16[16,5120]{1,0:T(8,128)(2,1)S(1)}, u32[]{:S(2)}, u32[]{:S(2)}) collective-permute-start(bf16[16,5120]{1,0:T(8,128)(2,1)S(1)} %pad_maximum_fusion.1), channel_id=1, source_target_pairs={{0,96},{32,0},{64,32},{96,64},{1,97},{33,1},{65,33},{97,65},{2,98}... | collective-permute-start | bytes 491528 | tf_op jit(solution)/shard_map/ppermute | solution.py:26
  129.1 13.0 %collective-permute-start.14 = (bf16[64,5120]{1,0:T(8,128)(2,1)}, bf16[64,5120]{1,0:T(8,128)(2,1)S(1)}, u32[]{:S(2)}, u32[]{:S(2)}) collective-permute-start(bf16[64,5120]{1,0:T(8,128)(2,1)} %constant_dynamic-update-slice_fusion.refs_0_), channel_id=1, source_target_pairs={{0,32},{32,64},{64,96},{96,0},{1,33},{33,65},{65,97},{97,1},{2,34}... | collective-permute-start | bytes 1966088 | tf_op jit(solution)/shard_map/ppermute | solution.py:26
  130.9 18.9 %collective-permute-start.15 = (bf16[64,5120]{1,0:T(8,128)(2,1)}, bf16[64,5120]{1,0:T(8,128)(2,1)}, u32[]{:S(2)}, u32[]{:S(2)}) collective-permute-start(bf16[64,5120]{1,0:T(8,128)(2,1)} %constant_dynamic-update-slice_fusion.refs_0_), channel_id=1, source_target_pairs={{0,96},{32,0},{64,32},{96,64},{1,97},{33,1},{65,33},{97,65},{2,98}... | collective-permute-start | bytes 1966088 | tf_op jit(solution)/shard_map/ppermute | solution.py:26
  142.1 22.3 %copy-start.4 = (bf16[64,5120]{1,0:T(8,128)(2,1)}, bf16[64,5120]{1,0:T(8,128)(2,1)S(1)}, u32[]{:S(2)}) copy-start(bf16[64,5120]{1,0:T(8,128)(2,1)S(1)} %collective-permute-done.14.refs_0_) | copy-start | bytes 1966084
  142.1 26.3 %collective-permute-start.16 = (bf16[64,5120]{1,0:T(8,128)(2,1)}, bf16[64,5120]{1,0:T(8,128)(2,1)}, u32[]{:S(2)}, u32[]{:S(2)}) collective-permute-start(bf16[64,5120]{1,0:T(8,128)(2,1)} %constant_dynamic-update-slice_fusion.5.refs_1_), channel_id=1, source_target_pairs={{0,8},{8,16},{16,24},{24,0},{1,9},{9,17},{17,25},{25,1},{2,10},{10... | collective-permute-start | bytes 1966088 | tf_op jit(solution)/shard_map/ppermute | solution.py:26
  149.7 21.7 %collective-permute-start.17 = (bf16[64,5120]{1,0:T(8,128)(2,1)}, bf16[64,5120]{1,0:T(8,128)(2,1)}, u32[]{:S(2)}, u32[]{:S(2)}) collective-permute-start(bf16[64,5120]{1,0:T(8,128)(2,1)} %constant_dynamic-update-slice_fusion.5.refs_1_), channel_id=1, source_target_pairs={{0,24},{8,0},{16,8},{24,16},{1,25},{9,1},{17,9},{25,17},{2,26},{10... | collective-permute-start | bytes 1966088 | tf_op jit(solution)/shard_map/ppermute | solution.py:26
  150.9 35.6 %collective-permute-start.21 = (bf16[64,5120]{1,0:T(8,128)(2,1)}, bf16[64,5120]{1,0:T(8,128)(2,1)}, u32[]{:S(2)}, u32[]{:S(2)}) collective-permute-start(bf16[64,5120]{1,0:T(8,128)(2,1)} %constant_dynamic-update-slice_fusion.refs_0_), channel_id=1, source_target_pairs={{0,64},{32,96},{64,0},{96,32},{1,65},{33,97},{65,1},{97,33},{2,66}... | collective-permute-start | bytes 1966088 | tf_op jit(solution)/shard_map/ppermute | solution.py:26
  150.9 38.3 %collective-permute-start.22 = (bf16[64,5120]{1,0:T(8,128)(2,1)}, bf16[64,5120]{1,0:T(8,128)(2,1)}, u32[]{:S(2)}, u32[]{:S(2)}) collective-permute-start(bf16[64,5120]{1,0:T(8,128)(2,1)} %constant_dynamic-update-slice_fusion.5.refs_1_), channel_id=1, source_target_pairs={{0,16},{8,24},{16,0},{24,8},{1,17},{9,25},{17,1},{25,9},{2,18},{10... | collective-permute-start | bytes 1966088 | tf_op jit(solution)/shard_map/ppermute | solution.py:26
  168.4 36.5 %collective-permute-start.11 = (bf16[128,512]{1,0:T(8,128)(2,1)}, bf16[128,512]{1,0:T(8,128)(2,1)S(1)}, u32[]{:S(2)}, u32[]{:S(2)}) collective-permute-start(bf16[128,512]{1,0:T(8,128)(2,1)} %mlp_in.3.refs_0_), channel_id=1, source_target_pairs={{0,1},{1,2},{2,3},{3,0},{4,5},{5,6},{6,7},{7,4},{8,9},{9,10},{10,1... | collective-permute-start | bytes 393224 | tf_op jit(solution)/shard_map/ppermute | solution.py:26
  171.4 34.3 %collective-permute-start.12 = (bf16[128,512]{1,0:T(8,128)(2,1)}, bf16[128,512]{1,0:T(8,128)(2,1)}, u32[]{:S(2)}, u32[]{:S(2)}) collective-permute-start(bf16[128,512]{1,0:T(8,128)(2,1)} %mlp_in.3.refs_0_), channel_id=1, source_target_pairs={{0,2},{1,3},{2,0},{3,1},{4,6},{5,7},{6,4},{7,5},{8,10},{9,11},{10,... | collective-permute-start | bytes 393224 | tf_op jit(solution)/shard_map/ppermute | solution.py:26
  186.5 20.5 %collective-permute-start.13 = (bf16[128,512]{1,0:T(8,128)(2,1)S(1)}, bf16[128,512]{1,0:T(8,128)(2,1)}, u32[]{:S(2)}, u32[]{:S(2)}) collective-permute-start(bf16[128,512]{1,0:T(8,128)(2,1)S(1)} %copy-done.5), channel_id=1, source_target_pairs={{0,3},{1,0},{2,1},{3,2},{4,7},{5,4},{6,5},{7,6},{8,11},{9,8},{10,9... | collective-permute-start | bytes 393224 | tf_op jit(solution)/shard_map/ppermute | solution.py:26
  189.3 28.1 %collective-permute-start.18 = (bf16[256,512]{1,0:T(8,128)(2,1)}, bf16[256,512]{1,0:T(8,128)(2,1)S(1)}, u32[]{:S(2)}, u32[]{:S(2)}) collective-permute-start(bf16[256,512]{1,0:T(8,128)(2,1)} %mlp_in.4.refs_4_), channel_id=1, source_target_pairs={{0,1},{1,2},{2,3},{3,0},{4,5},{5,6},{6,7},{7,4},{8,9},{9,10},{10,1... | collective-permute-start | bytes 786440 | tf_op jit(solution)/shard_map/ppermute | solution.py:26
  202.0 15.4 %collective-permute-start.19 = (bf16[256,512]{1,0:T(8,128)(2,1)S(1)}, bf16[256,512]{1,0:T(8,128)(2,1)}, u32[]{:S(2)}, u32[]{:S(2)}) collective-permute-start(bf16[256,512]{1,0:T(8,128)(2,1)S(1)} %copy-done.2), channel_id=1, source_target_pairs={{0,2},{1,3},{2,0},{3,1},{4,6},{5,7},{6,4},{7,5},{8,10},{9,11},{10,... | collective-permute-start | bytes 786440 | tf_op jit(solution)/shard_map/ppermute | solution.py:26
  204.9 12.5 %collective-permute-start.20 = (bf16[256,512]{1,0:T(8,128)(2,1)S(1)}, bf16[256,512]{1,0:T(8,128)(2,1)}, u32[]{:S(2)}, u32[]{:S(2)}) collective-permute-start(bf16[256,512]{1,0:T(8,128)(2,1)S(1)} %copy-done.2), channel_id=1, source_target_pairs={{0,3},{1,0},{2,1},{3,2},{4,7},{5,4},{6,5},{7,6},{8,11},{9,8},{10,9... | collective-permute-start | bytes 786440 | tf_op jit(solution)/shard_map/ppermute | solution.py:26
  205.6 6.5 %collective-permute-start.23 = (bf16[128,512]{1,0:T(8,128)(2,1)}, bf16[128,512]{1,0:T(8,128)(2,1)}, u32[]{:S(2)}, u32[]{:S(2)}) collective-permute-start(bf16[128,512]{1,0:T(8,128)(2,1)} %mlp_in.5.refs_8_), channel_id=1, source_target_pairs={{0,1},{1,2},{2,3},{3,0},{4,5},{5,6},{6,7},{7,4},{8,9},{9,10},{10,1... | collective-permute-start | bytes 393224 | tf_op jit(solution)/shard_map/ppermute | solution.py:26
  207.0 6.7 %collective-permute-start.24 = (bf16[128,512]{1,0:T(8,128)(2,1)}, bf16[128,512]{1,0:T(8,128)(2,1)S(1)}, u32[]{:S(2)}, u32[]{:S(2)}) collective-permute-start(bf16[128,512]{1,0:T(8,128)(2,1)} %mlp_in.5.refs_8_), channel_id=1, source_target_pairs={{0,2},{1,3},{2,0},{3,1},{4,6},{5,7},{6,4},{7,5},{8,10},{9,11},{10,... | collective-permute-start | bytes 393224 | tf_op jit(solution)/shard_map/ppermute | solution.py:26
  212.1 5.3 %collective-permute-start.25 = (bf16[128,512]{1,0:T(8,128)(2,1)}, bf16[128,512]{1,0:T(8,128)(2,1)}, u32[]{:S(2)}, u32[]{:S(2)}) collective-permute-start(bf16[128,512]{1,0:T(8,128)(2,1)} %mlp_in.5.refs_8_), channel_id=1, source_target_pairs={{0,3},{1,0},{2,1},{3,2},{4,7},{5,4},{6,5},{7,6},{8,11},{9,8},{10,9... | collective-permute-start | bytes 393224 | tf_op jit(solution)/shard_map/ppermute | solution.py:26
  (13 other events, 172.0 us)
